TPU v7x, 32 devices: a whole 2x2x4 slice. The times are simulated.
32 devices in a mesh: dp: 4 (over y, x), wide: 8 (over z, core).
Axes of the slice: x: 2, y: 2, z: 4, core: 2. Of those that a mesh axis runs over, the one named last changes fastest.
Arguments:
- tokens: bfloat16 [49152, 768], P(('dp', 'wide')), may hold values from -6 to 6
- cotangent: bfloat16 [49152, 768], P(('dp', 'wide')), may hold values from -6 to 6
- valid_token_length: int32 [224], P(('dp', 'wide')), may hold values from 1 to 512, as said below
- query_weight_matrix: bfloat16 [768, 768], replicated, may hold values from -0.21875 to 0.21875
- key_weight_matrix: bfloat16 [768, 768], replicated, may hold values from -0.21875 to 0.21875
- value_weight_matrix: bfloat16 [768, 768], replicated, may hold values from -0.21875 to 0.21875
- attention_output_weight: bfloat16 [768, 768], replicated, may hold values from -0.875 to 0.875
- inner_ffn_weight: bfloat16 [768, 3072], replicated, may hold values from -0.21875 to 0.21875
- outer_ffn_weight: bfloat16 [3072, 768], replicated, may hold values from -0.109375 to 0.109375
- query_bias_vector: float32 [768], replicated, may hold values from -1.8 to 1.8
- value_bias_vector: float32 [768], replicated, may hold values from -1.8 to 1.8
- attention_output_bias: float32 [768], replicated, may hold values from -1.8 to 1.8
- hidden_ffn_bias: float32 [3072], replicated, may hold values from -1.8 to 1.8
- ffn_output_bias: float32 [768], replicated, may hold values from -1.8 to 1.8
- layer_norm_gains: float32 [2, 768], replicated, may hold values from 0.5 to 1.5
- layer_norm_biases: float32 [2, 768], replicated, may hold values from -1.8 to 1.8
- adapter_down_factors: float32 [2, 768, 8], replicated, may hold values from -0.21875 to 0.21875
- adapter_up_factors: float32 [2, 8, 768], replicated, may hold values from -0.3 to 0.3
- first_moment_estimate: float32 [24576], P('wide'), may hold values from -0.0005412659 to 0.0005412659
- second_moment_estimate: float32 [24576], P('wide'), may hold values from 4.0690104e-10 to 4.0690105e-09
- first_decay_factor: float32 [1], replicated, may hold values from 0.85 to 0.95
- second_decay_factor: float32 [1], replicated, may hold values from 0.998 to 0.9995
- optimizer_step_number: int32 [1], replicated, may hold values from 1 to 1024
Outputs:
- mixed: bfloat16 [49152, 768], P(('dp', 'wide'))
- input_token_gradient: bfloat16 [49152, 768], P(('dp', 'wide'))
- updated_down_factors: float32 [2, 768, 8], replicated
- updated_up_factors: float32 [2, 8, 768], replicated
- updated_first_moment: float32 [24576], P('wide')
- updated_second_moment: float32 [24576], P('wide')
Inputs may be any that keep to these rules, and one draw needn't show every extreme that they name: `valid_token_length`: entry n * 7 + s belongs to sequence s of device n (dp slowest); sequences 0 to 3 of a device have 128 slots, the next 2 have 256, the last 1 have 512; every entry is at most its sequence's slots.
All inputs are finite; a program needn't handle non-finite values.
Results may differ from a plain program's by a relative error of at most 0.035.
Values sent between devices are 32-bit elements; how exact they have to be, the bound alone decides.
No kernel may reach another device: no remote copies, remote signals or barrier semaphores. Data moves between devices by JAX's collectives and lax.ppermute only.
A program may use at most 192 MiB of HBM per device.

v0:
```python
import jax
import jax.numpy as jnp
from jax import lax
from jax.experimental import pallas as pl
from jax.experimental.pallas import tpu as pltpu
from jax.sharding import PartitionSpec as P

HEADS = 12
HEAD_DIM = 64
LEN_A = 128
LEN_B = 256
LEN_C = 512
BUCKET = 512
LANES = 128

adapter_scale = 2.0
rate_first = 0.005
rate_second = 0.08
decay_first = 0.05
decay_second = 0.01
neg_large = -1e30
norm_eps = 1e-05
adam_eps = 1e-08

f32 = jnp.float32
bf16 = jnp.bfloat16
sds = jax.ShapeDtypeStruct
VMEM = pltpu.VMEM


def cdot(left, right, left_dim, right_dim, precision=None):
    return lax.dot_general(
        left,
        right,
        (((left_dim,), (right_dim,)), ((), ())),
        precision=precision,
        preferred_element_type=f32,
    )


def low_lanes(shape):
    return lax.broadcasted_iota(jnp.int32, shape, 1) < HEAD_DIM


def head_pair_rows(pair, with_ones):
    low = low_lanes(pair.shape)
    zero = jnp.zeros_like(pair)
    first = jnp.where(low, pair, zero)
    second = jnp.where(low, zero, pair)
    if with_ones:
        one = jnp.ones_like(pair)
        first = jnp.concatenate([first, jnp.where(low, one, zero)], axis=1)
        second = jnp.concatenate([second, jnp.where(low, zero, one)], axis=1)
    return jnp.concatenate([first, second], axis=0)


def row_mean(values):
    return jnp.sum(values, axis=1, keepdims=True) * (1.0 / values.shape[1])


def layer_kernel(
    lens,
    x_hbm,
    cot_hbm,
    wq_hbm,
    wk_hbm,
    wv_hbm,
    wo_hbm,
    w1_hbm,
    w2_hbm,
    bq,
    bv,
    bo,
    b1,
    b2,
    gains,
    shifts,
    down,
    up,
    mixed_hbm,
    midg_hbm,
    dq_hbm,
    dk_hbm,
    dv_hbm,
    dg_hbm,
    keep_out,
    send_out,
    x,
    cot,
    wq,
    wk,
    wv,
    wo,
    w1,
    w2,
    acat,
    bcat_q,
    bcat_v,
    brep_q,
    brep_v,
    rowv,
    qs,
    ks,
    vs,
    dn,
    probs,
    ctx,
    inv_l,
    dctx,
    act,
    slope,
    mixed,
    midg,
    dq,
    dk,
    dv,
    dg,
    g_down,
    g_up_q,
    g_up_v,
    flat,
    in_sem,
    w_sem,
    out_sem,
    *,
    wide,
):
    d_model = x.shape[1]
    n_bucket = x.shape[0] // BUCKET
    n_pair = d_model // LANES
    ff = w1.shape[1]
    rank = up.shape[1]

    def bucket_copy(i, src, dst, sem):
        rows = pl.ds(i * BUCKET, BUCKET)
        return pltpu.make_async_copy(src.at[rows, :], dst.at[rows, :], sem)

    weights = [(wq_hbm, wq), (wk_hbm, wk), (wv_hbm, wv), (wo_hbm, wo), (w1_hbm, w1), (w2_hbm, w2)]
    weight_copies = [pltpu.make_async_copy(s, d, w_sem.at[i]) for i, (s, d) in enumerate(weights)]
    x_copies = [bucket_copy(i, x_hbm, x, in_sem.at[i]) for i in range(n_bucket)]
    cot_copies = [bucket_copy(i, cot_hbm, cot, in_sem.at[n_bucket + i]) for i in range(n_bucket)]
    x_copies[0].start()
    for c in weight_copies[:4]:
        c.start()
    cot_copies[0].start()
    for c in weight_copies[4:]:
        c.start()
    for c in x_copies[1:] + cot_copies[1:]:
        c.start()

    down_q = down[0].astype(bf16)
    down_v = down[1].astype(bf16)
    r_i = lax.broadcasted_iota(jnp.int32, (rank, LANES), 0)
    l_i = lax.broadcasted_iota(jnp.int32, (rank, LANES), 1)
    acat[...] = (
        cdot(down_q, (l_i == r_i).astype(bf16), 1, 0)
        + cdot(down_v, (l_i == r_i + rank).astype(bf16), 1, 0)
    ).astype(bf16)
    up_q = up[0].astype(bf16).astype(f32) * adapter_scale
    up_v = up[1].astype(bf16).astype(f32) * adapter_scale
    bcat_q[...] = jnp.concatenate(
        [up_q, jnp.zeros((LANES - rank, d_model), f32)], axis=0
    ).astype(bf16)
    bcat_v[...] = jnp.concatenate(
        [jnp.zeros((rank, d_model), f32), up_v, jnp.zeros((LANES - 2 * rank, d_model), f32)], axis=0
    ).astype(bf16)
    brep_q[...] = jnp.concatenate([up_q] * (LANES // rank), axis=0).astype(bf16)
    brep_v[...] = jnp.concatenate([up_v] * (LANES // rank), axis=0).astype(bf16)
    seq = 0
    row0 = 0
    n_valid = 0
    for length in (LEN_A, LEN_B, LEN_C):
        for s in range(BUCKET // length):
            n = lens[seq]
            n_valid = n_valid + n
            rowv[row0 : row0 + length, :] = (
                lax.broadcasted_iota(jnp.int32, (length, LANES), 0) < n
            ).astype(f32)
            seq += 1
            row0 += length
    g_down[...] = jnp.zeros_like(g_down)
    g_up_q[...] = jnp.zeros_like(g_up_q)
    g_up_v[...] = jnp.zeros_like(g_up_v)

    def attend(length, first_seq, b, p, s):
        rows = slice(s * length, (s + 1) * length)
        cols = pl.ds(pl.multiple_of(p * LANES, LANES), LANES)
        key_rows = head_pair_rows(ks[rows, cols], False)
        val_rows = head_pair_rows(vs[rows, cols], True)
        lane = lax.broadcasted_iota(jnp.int32, (1, length), 1)
        bias = jnp.where(lane < lens[first_seq + s], 0.0, neg_large).astype(f32)
        scores = cdot(qs[rows, cols], key_rows, 1, 1)
        parts = []
        for h in range(2):
            sh = scores[:, h * length : (h + 1) * length] + bias
            parts.append(jnp.exp(sh - jnp.max(sh, axis=1, keepdims=True)).astype(bf16))
        e = jnp.concatenate(parts, axis=1)
        probs[pl.ds(pl.multiple_of(p * BUCKET + s * length, LANES), length), : 2 * length] = e
        out = cdot(e, val_rows, 1, 0)
        inv = 1.0 / out[:, LANES:]
        inv_l[rows, cols] = inv
        ctx[rows, cols] = (out[:, :LANES] * inv).astype(bf16)

    def attend_back(length, b, p, s):
        rows = slice(s * length, (s + 1) * length)
        grows = pl.ds(pl.multiple_of(b * BUCKET + s * length, LANES), length)
        cols = pl.ds(pl.multiple_of(p * LANES, LANES), LANES)
        key_rows = head_pair_rows(ks[rows, cols], False)
        val_rows = head_pair_rows(vs[rows, cols], True)
        dcf = dctx[rows, cols].astype(f32) * inv_l[rows, cols]
        dc = dcf.astype(bf16)
        inner = (-dcf * ctx[rows, cols].astype(f32)).astype(bf16)
        g = cdot(jnp.concatenate([dc, inner], axis=1), val_rows, 1, 1)
        e = probs[pl.ds(pl.multiple_of(p * BUCKET + s * length, LANES), length), : 2 * length]
        ds = (e.astype(f32) * g).astype(bf16)
        dq[grows, cols] = (cdot(ds, key_rows, 1, 0) * (HEAD_DIM**-0.5)).astype(bf16)
        low = low_lanes((length, LANES))
        rk = cdot(ds, qs[rows, cols], 0, 0)
        dk[grows, cols] = jnp.where(low, rk[:length], rk[length:]).astype(bf16)
        rv = cdot(e, dc, 0, 0)
        dv[grows, cols] = jnp.where(low, rv[:length], rv[length:]).astype(bf16)

    def chain(b, c):
        size = 256
        lrows = pl.ds(pl.multiple_of(c * size, size), size)
        grows = pl.ds(pl.multiple_of(b * BUCKET + c * size, size), size)
        ms = cdot(ctx[lrows, :], wo[...], 1, 0) + bo[...] + x[grows, :].astype(f32)
        xc = ms - row_mean(ms)
        r1 = lax.rsqrt(row_mean(xc * xc) + norm_eps)
        n1 = xc * r1
        normed = n1 * gains[0:1, :] + shifts[0:1, :]
        nl = normed.astype(bf16)
        step = 512
        for n in range(0, ff, step):
            h = cdot(nl, w1[:, n : n + step], 1, 0) + b1[:, n : n + step]
            cdf = 0.5 + 0.5 * lax.erf(h * (0.5**0.5))
            pdf = jnp.exp(h * h * -0.5) * 0.3989422804014327
            act[:, n : n + step] = (h * cdf).astype(bf16)
            slope[:, n : n + step] = (cdf + h * pdf).astype(bf16)
        fs = cdot(act[...], w2[...], 1, 0) + b2[...] + normed
        fc = fs - row_mean(fs)
        r2 = lax.rsqrt(row_mean(fc * fc) + norm_eps)
        n2 = fc * r2
        mixed[grows, :] = (n2 * gains[1:2, :] + shifts[1:2, :]).astype(bf16)
        rv = rowv[grows, :]
        e2 = cot[grows, :].astype(f32) * jnp.concatenate([rv] * n_pair, axis=1) * gains[1:2, :]
        fg = r2 * (e2 - row_mean(e2) - n2 * row_mean(e2 * n2))
        ol = fg.astype(bf16)
        for n in range(0, ff, step):
            da = cdot(ol, w2[n : n + step, :], 1, 1)
            act[:, n : n + step] = (
                da.astype(bf16).astype(f32) * slope[:, n : n + step].astype(f32)
            ).astype(bf16)
        ng = fg + cdot(act[...], w1[...], 1, 1)
        e1 = ng * gains[0:1, :]
        mg = r1 * (e1 - row_mean(e1) - n1 * row_mean(e1 * n1))
        midg[grows, :] = mg
        dctx[lrows, :] = cdot(mg.astype(bf16), wo[...], 1, 1).astype(bf16)

    outs = [
        (mixed, mixed_hbm),
        (midg, midg_hbm),
        (dq, dq_hbm),
        (dk, dk_hbm),
        (dv, dv_hbm),
        (dg, dg_hbm),
    ]

    def bucket(b, carry):
        rows = pl.ds(pl.multiple_of(b * BUCKET, BUCKET), BUCKET)

        def wait_bucket(src, dst, base):
            pltpu.make_async_copy(src.at[rows, :], dst.at[rows, :], in_sem.at[base + b]).wait()

        wait_bucket(x_hbm, x, 0)

        @pl.when(b == 0)
        def _():
            for c in weight_copies[:3]:
                c.wait()

        xb = x[rows, :]
        dnb = cdot(xb, acat[...], 1, 0).astype(bf16)
        dn[...] = dnb
        qs[...] = (
            (cdot(xb, wq[...], 1, 0) + bq[...] + cdot(dnb, bcat_q[...], 1, 0)).astype(bf16)
            * jnp.asarray(HEAD_DIM**-0.5, bf16)
        )
        ks[...] = cdot(xb, wk[...], 1, 0).astype(bf16)
        vs[...] = (cdot(xb, wv[...], 1, 0) + bv[...] + cdot(dnb, bcat_v[...], 1, 0)).astype(bf16)

        first = 0
        for i, length in enumerate((LEN_A, LEN_B, LEN_C)):
            count = BUCKET // length

            @pl.when(b == i)
            def _(length=length, first=first, count=count):
                def pair(p, carry):
                    for s in range(count):
                        attend(length, first, b, p, s)
                    return carry

                lax.fori_loop(0, n_pair, pair, 0)

            first += count

        wait_bucket(cot_hbm, cot, n_bucket)

        @pl.when(b == 0)
        def _():
            for c in weight_copies[3:]:
                c.wait()

        def chunk(c, carry):
            chain(b, c)
            return carry

        lax.fori_loop(0, 2, chunk, 0)

        for i, length in enumerate((LEN_A, LEN_B, LEN_C)):
            count = BUCKET // length

            @pl.when(b == i)
            def _(length=length, count=count):
                def pair(p, carry):
                    for s in range(count):
                        attend_back(length, b, p, s)
                    return carry

                lax.fori_loop(0, n_pair, pair, 0)

        dqb = dq[rows, :]
        dvb = dv[rows, :]
        dgb = jnp.concatenate(
            [cdot(dqb, brep_q[...], 1, 1).astype(bf16), cdot(dvb, brep_v[...], 1, 1).astype(bf16)],
            axis=1,
        )
        dg[rows, :] = dgb
        g_down[...] += cdot(x[rows, :], dgb, 0, 0)
        dnb2 = dn[...]
        g_up_q[...] += cdot(dnb2, dqb, 0, 0)
        g_up_v[...] += cdot(dnb2, dvb, 0, 0)
        for i, (src, dst) in enumerate(outs):
            pltpu.make_async_copy(src.at[rows, :], dst.at[rows, :], out_sem.at[i * n_bucket + b]).start()
        return carry

    lax.fori_loop(0, n_bucket, bucket, 0)

    group = LANES // rank
    half_rows = d_model // group
    up_rows = d_model // LANES
    row_i = lax.broadcasted_iota(jnp.int32, (d_model, LANES), 0)
    lane_i = lax.broadcasted_iota(jnp.int32, (d_model, LANES), 1)
    pick = (row_i % group) == (lane_i // rank)
    for j in range(2):
        part = jnp.where(pick, g_down[:, j * LANES : (j + 1) * LANES], 0.0)
        flat[j * half_rows : (j + 1) * half_rows, :] = jnp.sum(
            part.reshape(half_rows, group, LANES), axis=1
        )
        src = (g_up_q, g_up_v)[j]
        base = 2 * half_rows + j * rank * up_rows
        for cb in range(up_rows):
            flat[pl.ds(base + cb, rank, stride=up_rows), :] = adapter_scale * (
                src[j * rank : (j + 1) * rank, cb * LANES : (cb + 1) * LANES]
            )
    core = lax.rem(lax.axis_index("wide"), 2)
    n_rows = flat.shape[0]
    chunk_rows = n_rows // wide
    unit = 8 if chunk_rows % 8 == 0 else 1
    for h in range(wide // 2):
        for k in range(0, chunk_rows, unit):
            at = h * chunk_rows + k
            mine = 2 * h * chunk_rows + k + core * chunk_rows
            other = 2 * h * chunk_rows + k + (1 - core) * chunk_rows
            if unit == 8:
                mine = pl.multiple_of(mine, 8)
                other = pl.multiple_of(other, 8)
            keep_out[at : at + unit, :] = flat[pl.ds(mine, unit), :]
            send_out[at : at + unit, :] = flat[pl.ds(other, unit), :]
    total = jnp.full((8, LANES), n_valid, jnp.int32).astype(f32)
    keep_out[n_rows // 2 :, :] = total
    send_out[n_rows // 2 :, :] = total
    for i, (src, dst) in enumerate(outs):
        for j in range(n_bucket):
            bucket_copy(j, src, dst, out_sem.at[i * n_bucket + j]).wait()


def layer(lens, x, cot, ws, vecs, gains, shifts, down, up, wide):
    t, d = x.shape
    ff = ws[4].shape[1]
    rank = up.shape[1]
    n_rows = 2 * down.size // LANES
    n_bucket = t // BUCKET
    any_spec = pl.BlockSpec(memory_space=pl.ANY)
    vm = pl.BlockSpec(memory_space=VMEM)
    ops = [lens, x, cot, *ws, *vecs, gains, shifts, down, up]
    in_specs = (
        [pl.BlockSpec(memory_space=pltpu.SMEM)] + [any_spec] * 8 + [vm] * (len(vecs) + 4)
    )
    out_shape = [
        sds((t, d), bf16),
        sds((t, d), f32),
        sds((t, d), bf16),
        sds((t, d), bf16),
        sds((t, d), bf16),
        sds((t, 2 * LANES), bf16),
        sds((n_rows // 2 + 8, LANES), f32),
        sds((n_rows // 2 + 8, LANES), f32),
    ]
    dma = pltpu.SemaphoreType.DMA
    scratch = [
        VMEM((t, d), bf16),
        VMEM((t, d), bf16),
        VMEM((d, d), bf16),
        VMEM((d, d), bf16),
        VMEM((d, d), bf16),
        VMEM((d, d), bf16),
        VMEM((d, ff), bf16),
        VMEM((ff, d), bf16),
        VMEM((d, LANES), bf16),
        VMEM((LANES, d), bf16),
        VMEM((LANES, d), bf16),
        VMEM((LANES, d), bf16),
        VMEM((LANES, d), bf16),
        VMEM((t, LANES), f32),
        VMEM((BUCKET, d), bf16),
        VMEM((BUCKET, d), bf16),
        VMEM((BUCKET, d), bf16),
        VMEM((BUCKET, LANES), bf16),
        VMEM((d // LANES * BUCKET, 2 * LEN_C), bf16),
        VMEM((BUCKET, d), bf16),
        VMEM((BUCKET, d), f32),
        VMEM((BUCKET, d), bf16),
        VMEM((256, ff), bf16),
        VMEM((256, ff), bf16),
        VMEM((t, d), bf16),
        VMEM((t, d), f32),
        VMEM((t, d), bf16),
        VMEM((t, d), bf16),
        VMEM((t, d), bf16),
        VMEM((t, 2 * LANES), bf16),
        VMEM((d, 2 * LANES), f32),
        VMEM((LANES, d), f32),
        VMEM((LANES, d), f32),
        VMEM((n_rows, LANES), f32),
        dma((2 * n_bucket,)),
        dma((6,)),
        dma((6 * n_bucket,)),
    ]
    body = lambda *refs: layer_kernel(*refs, wide=wide)
    return pl.pallas_call(
        body,
        out_shape=out_shape,
        in_specs=in_specs,
        out_specs=[any_spec] * 6 + [vm] * 2,
        scratch_shapes=scratch,
        compiler_params=pltpu.CompilerParams(vmem_limit_bytes=63 << 20),
        name="layer",
    )(*ops)


def token_kernel(mg, dq, dk, dv, dg, wq, wk, wv, down, out):
    down_q = down[0].astype(bf16)
    down_v = down[1].astype(bf16)
    acc = mg[...] + cdot(dq[...], wq[...], 1, 1)
    acc = acc + cdot(dk[...], wk[...], 1, 1)
    acc = acc + cdot(dv[...], wv[...], 1, 1)
    rank = down.shape[2]
    acc = acc + cdot(dg[:, :rank], down_q, 1, 1)
    acc = acc + cdot(dg[:, LANES : LANES + rank], down_v, 1, 1)
    out[...] = acc.astype(bf16)


def token_gradient(mg, dq, dk, dv, dg, wq, wk, wv, down):
    t, d = mg.shape
    size = 256
    row = lambda i: (i, 0)
    fixed = lambda i: (0, 0)
    return pl.pallas_call(
        token_kernel,
        grid=(t // size,),
        out_shape=sds((t, d), bf16),
        in_specs=[
            pl.BlockSpec((size, d), row),
            pl.BlockSpec((size, d), row),
            pl.BlockSpec((size, d), row),
            pl.BlockSpec((size, d), row),
            pl.BlockSpec((size, 2 * LANES), row),
            pl.BlockSpec((d, d), fixed),
            pl.BlockSpec((d, d), fixed),
            pl.BlockSpec((d, d), fixed),
            pl.BlockSpec(down.shape, lambda i: (0, 0, 0)),
        ],
        out_specs=pl.BlockSpec((size, d), row),
        compiler_params=pltpu.CompilerParams(vmem_limit_bytes=24 << 20),
        cost_estimate=pl.CostEstimate(
            flops=6 * t * d * d, bytes_accessed=14 * t * d, transcendentals=0
        ),
        name="token_gradient",
    )(mg, dq, dk, dv, dg, wq, wk, wv, down)


def digit_groups(size, first):
    bits = size.bit_length() - 1
    groups = []
    at = first
    while at < bits:
        n = min(2, bits - at)
        groups.append((at, n))
        at += n
    return groups


def swap_perm(size, mask):
    return [(i, i ^ mask) for i in range(size)]


def exchange(values, axis, size, group):
    low, n = group
    return [values] + [
        lax.ppermute(values, axis, swap_perm(size, j << low)) for j in range(1, 1 << n)
    ]


def tree_sum(parts):
    while len(parts) > 1:
        parts = [parts[i] + parts[i + 1] for i in range(0, len(parts), 2)]
    return parts[0]


def in_order(parts, digit):
    parts = list(parts)
    n = len(parts).bit_length() - 1
    for bit in range(n):
        flip = (digit >> bit) & 1
        parts = [jnp.where(flip == 1, parts[i ^ (1 << bit)], parts[i]) for i in range(len(parts))]
    return parts


def per_device(
    tokens,
    cotangent,
    valid_token_length,
    query_weight_matrix,
    key_weight_matrix,
    value_weight_matrix,
    attention_output_weight,
    inner_ffn_weight,
    outer_ffn_weight,
    query_bias_vector,
    value_bias_vector,
    attention_output_bias,
    hidden_ffn_bias,
    ffn_output_bias,
    layer_norm_gains,
    layer_norm_biases,
    adapter_down_factors,
    adapter_up_factors,
    first_moment_estimate,
    second_moment_estimate,
    first_decay_factor,
    second_decay_factor,
    optimizer_step_number,
):
    dp = lax.axis_size("dp")
    wide = lax.axis_size("wide")
    place = lax.axis_index("wide")
    core = place % 2
    n_rows = 2 * adapter_down_factors.size // LANES
    chunk_rows = n_rows // wide

    moments = jnp.concatenate(
        [first_moment_estimate.reshape(chunk_rows, LANES), second_moment_estimate.reshape(chunk_rows, LANES)],
        axis=0,
    )[None]
    for low, n in digit_groups(wide, 1):
        parts = exchange(moments, "wide", wide, (low, n))
        moments = jnp.concatenate(in_order(parts, place >> low), axis=0)
    first_half = moments[:, :chunk_rows].reshape(n_rows // 2, LANES)
    second_half = moments[:, chunk_rows:].reshape(n_rows // 2, LANES)

    params = jnp.concatenate(
        [adapter_down_factors.reshape(-1), adapter_up_factors.reshape(-1)]
    ).reshape(wide // 2, 2, chunk_rows, LANES)
    own_params = lax.dynamic_index_in_dim(params, core, 1, keepdims=False).reshape(n_rows // 2, LANES)

    mixed, midg, dq, dk, dv, dg, keep, send = layer(
        valid_token_length,
        tokens,
        cotangent,
        (
            query_weight_matrix,
            key_weight_matrix,
            value_weight_matrix,
            attention_output_weight,
            inner_ffn_weight,
            outer_ffn_weight,
        ),
        tuple(
            v.reshape(1, -1)
            for v in (
                query_bias_vector,
                value_bias_vector,
                attention_output_bias,
                hidden_ffn_bias,
                ffn_output_bias,
            )
        ),
        layer_norm_gains,
        layer_norm_biases,
        adapter_down_factors,
        adapter_up_factors,
        wide,
    )

    grad = keep + lax.ppermute(send, "wide", swap_perm(wide, 1))
    for group in digit_groups(dp, 0):
        grad = tree_sum(exchange(grad, "dp", dp, group))
    for group in digit_groups(wide, 1):
        grad = tree_sum(exchange(grad, "wide", wide, group))

    input_token_gradient = token_gradient(
        midg,
        dq,
        dk,
        dv,
        dg,
        query_weight_matrix,
        key_weight_matrix,
        value_weight_matrix,
        adapter_down_factors,
    )

    count = grad[n_rows // 2, 0]
    gradient = grad[: n_rows // 2] / count
    beta_one = first_decay_factor[0]
    beta_two = second_decay_factor[0]
    step = optimizer_step_number[0].astype(f32)
    inside_first = lax.broadcasted_iota(jnp.int32, (n_rows // 2, LANES), 0) < n_rows // 4
    step_rate = jnp.where(inside_first, rate_first, rate_second)
    decay_rate = jnp.where(inside_first, decay_first, decay_second)
    new_first = beta_one * first_half + (1.0 - beta_one) * gradient
    new_second = beta_two * second_half + (1.0 - beta_two) * gradient * gradient
    first_hat = new_first / (1.0 - jnp.power(beta_one, step))
    second_hat = new_second / (1.0 - jnp.power(beta_two, step))
    new_params = own_params * (1.0 - step_rate * decay_rate) - step_rate * first_hat / (
        jnp.sqrt(second_hat) + adam_eps
    )
    own = (place // 2) * chunk_rows
    updated_first = lax.dynamic_slice_in_dim(new_first, own, chunk_rows, 0).reshape(-1)
    updated_second = lax.dynamic_slice_in_dim(new_second, own, chunk_rows, 0).reshape(-1)
    other_params = lax.ppermute(new_params, "wide", swap_perm(wide, 1))
    halves = [
        v.reshape(wide // 2, 1, chunk_rows, LANES) for v in in_order([new_params, other_params], core)
    ]
    whole = jnp.concatenate(halves, axis=1).reshape(-1)
    updated_down = whole[: adapter_down_factors.size].reshape(adapter_down_factors.shape)
    updated_up = whole[adapter_down_factors.size :].reshape(adapter_up_factors.shape)
    return (mixed, input_token_gradient, updated_down, updated_up, updated_first, updated_second)


def solution(mesh):
    rows = P(("dp", "wide"), None)
    placed = (rows, rows, P(("dp", "wide"))) + (P(),) * 15 + (P("wide"), P("wide")) + (P(),) * 3
    return jax.shard_map(
        per_device,
        mesh=mesh,
        in_specs=placed,
        out_specs=(rows, rows, P(), P(), P("wide"), P("wide")),
        check_vma=False,
    )
```

profile of v0, /device:TPU:1, one launch (start us, length us, event | category | flops | bytes accessed | tf_op | source)
XLA Modules:
  0.0 157.3 jit_solution(1758021592141643860)
XLA Ops:
  1.4 4.2 %collective-permute-start = (f32[1,48,128]{2,1,0:T(8,128)S(1)}, f32[1,48,128]{2,1,0:T(8,128)S(1)}, u32[]{:S(2)}, u32[]{:S(2)}) collective-permute-start(f32[1,48,128]{2,1,0:T(8,128)S(1)} %maximum_bitcast_fusion), channel_id=1, source_target_pairs={{0,6},{1,7},{2,4},{3,5},{4,2},{5,3},{6,0},{7,1},{8,14},{9,15},{10,... | collective-permute-start | bytes 73736 | tf_op jit(solution)/shard_map/ppermute | solution.py:521
  5.8 1.3 reshape.74.refs_9_
  7.1 1.3 reshape.75.refs_10_
  8.3 1.3 reshape.76.refs_11_
  9.6 1.3 reshape.78.refs_13_
  10.9 1.9 %copy.33.refs_16_.down = f32[2,768,8]{2,1,0:T(8,128)} copy(f32[2,768,8]{1,2,0:T(8,128)} %param.39) | data formatting | bytes 98304 | tf_op args[16]
  12.8 99.3 %layer.1 = (bf16[1536,768]{1,0:T(8,128)(2,1)}, f32[1536,768]{1,0:T(8,128)}, bf16[1536,768]{1,0:T(8,128)(2,1)}, bf16[1536,768]{1,0:T(8,128)(2,1)}, bf16[1536,768]...) custom-call(s32[7]{0:T(128)} %refs_0_.1, bf16[1536,768]{1,0:T(8,128)(2,1)} %refs_1_.1, ...), custom_call_target="tpu_custom_call" | custom-call | tf_op jit(solution)/shard_map/layer/pallas_call | solution.py:451
  112.1 1.3 collective-permute-start.3
  113.9 1.3 copy-done.1
  115.1 1.3 copy-done.2
  116.4 1.3 copy-done.3
  117.7 2.3 %copy-done.4 = f32[1536,768]{1,0:T(8,128)S(1)} copy-done((f32[1536,768]{1,0:T(8,128)S(1)}, f32[1536,768]{1,0:T(8,128)}, u32[]{:S(2)}) %copy-start.4) | copy-done | bytes 4718616
  120.0 1.7 %copy-done.5 = bf16[1536,768]{1,0:T(8,128)(2,1)S(1)} copy-done((bf16[1536,768]{1,0:T(8,128)(2,1)S(1)}, bf16[1536,768]{1,0:T(8,128)(2,1)}, u32[]{:S(2)}) %copy-start.5) | copy-done | bytes 2359320
  121.7 1.7 %copy-done.6 = bf16[1536,768]{1,0:T(8,128)(2,1)S(1)} copy-done((bf16[1536,768]{1,0:T(8,128)(2,1)S(1)}, bf16[1536,768]{1,0:T(8,128)(2,1)}, u32[]{:S(2)}) %copy-start.6) | copy-done | bytes 2359320
  123.3 1.7 %copy-done.7 = bf16[1536,768]{1,0:T(8,128)(2,1)S(1)} copy-done((bf16[1536,768]{1,0:T(8,128)(2,1)S(1)}, bf16[1536,768]{1,0:T(8,128)(2,1)}, u32[]{:S(2)}) %copy-start.7) | copy-done | bytes 2359320
  125.0 1.1 copy-done.8
  126.1 8.9 %token_gradient.1 = bf16[1536,768]{1,0:T(8,128)(2,1)} custom-call(f32[1536,768]{1,0:T(8,128)S(1)} %copy-done.4, bf16[1536,768]{1,0:T(8,128)(2,1)S(1)} %copy-done.5, bf16[1536,768]{1,0:T(8,128)(2,1)S(1)} %copy-done.6, bf16[1536,768]{1,0:T(8,128)(2,1)S(1)} %copy-done.7, bf16[1536,256]{1,0:T(8,128)(2,1)S(1)} %copy-done.8, bf16[768,768]{1,0:T(8,128)(2,1)S(1)} %copy-done.1, ...), custom_call_target="tpu_custom_call" | custom-call | flops 5435817984 | bytes 16515072 | tf_op jit(solution)/shard_map/token_gradient/pallas_call | solution.py:479
  137.2 1.5 collective-permute-start.5
  138.7 1.2 collective-permute-start.6
  140.6 2.0 %collective-permute-done.6 = f32[104,128]{1,0:T(8,128)S(1)} collective-permute-done((f32[104,128]{1,0:T(8,128)S(1)}, f32[104,128]{1,0:T(8,128)S(1)}, u32[]{:S(2)}, u32[]{:S(2)}) %collective-permute-start.6) | collective-permute-done | bytes 53280 | tf_op jit(solution)/shard_map/ppermute | solution.py:521
  143.2 2.1 %collective-permute-start.8 = (f32[104,128]{1,0:T(8,128)S(1)}, f32[104,128]{1,0:T(8,128)S(1)}, u32[]{:S(2)}, u32[]{:S(2)}) collective-permute-start(f32[104,128]{1,0:T(8,128)S(1)} %add_add_fusion.1), channel_id=1, source_target_pairs={{0,4},{1,5},{2,6},{3,7},{4,0},{5,1},{6,2},{7,3},{8,12},{9,13},{10,... | collective-permute-start | bytes 159752 | tf_op jit(solution)/shard_map/ppermute | solution.py:521
  145.3 1.5 collective-permute-start.9
  147.1 3.3 %collective-permute-done.9 = f32[104,128]{1,0:T(8,128)S(1)} collective-permute-done((f32[104,128]{1,0:T(8,128)S(1)}, f32[104,128]{1,0:T(8,128)S(1)}, u32[]{:S(2)}, u32[]{:S(2)}) %collective-permute-start.9) | collective-permute-done | bytes 53280 | tf_op jit(solution)/shard_map/ppermute | solution.py:521
  151.7 2.7 %collective-permute-start.10 = (f32[96,128]{1,0:T(8,128)S(1)}, f32[96,128]{1,0:T(8,128)S(1)}, u32[]{:S(2)}, u32[]{:S(2)}) collective-permute-start(f32[96,128]{1,0:T(8,128)S(1)} %get-tuple-element.28), channel_id=1, source_target_pairs={{0,1},{1,0},{2,3},{3,2},{4,5},{5,4},{6,7},{7,6},{8,9},{9,8},{10,11... | collective-permute-start | bytes 147464 | tf_op jit(solution)/shard_map/ppermute | solution.py:652
  (51 shorter events, 7.2 us)
Async XLA Ops:
  1.4 135.7 %collective-permute-start = (f32[1,48,128]{2,1,0:T(8,128)S(1)}, f32[1,48,128]{2,1,0:T(8,128)S(1)}, u32[]{:S(2)}, u32[]{:S(2)}) collective-permute-start(f32[1,48,128]{2,1,0:T(8,128)S(1)} %maximum_bitcast_fusion), channel_id=1, source_target_pairs={{0,6},{1,7},{2,4},{3,5},{4,2},{5,3},{6,0},{7,1},{8,14},{9,15},{10,... | collective-permute-start | bytes 73736 | tf_op jit(solution)/shard_map/ppermute | solution.py:521
  5.5 131.6 %collective-permute-start.1 = (f32[1,48,128]{2,1,0:T(8,128)S(1)}, f32[1,48,128]{2,1,0:T(8,128)S(1)}, u32[]{:S(2)}, u32[]{:S(2)}) collective-permute-start(f32[1,48,128]{2,1,0:T(8,128)S(1)} %maximum_bitcast_fusion), channel_id=1, source_target_pairs={{0,4},{1,5},{2,6},{3,7},{4,0},{5,1},{6,2},{7,3},{8,12},{9,13},{10,... | collective-permute-start | bytes 73736 | tf_op jit(solution)/shard_map/ppermute | solution.py:521
  5.5 131.6 %collective-permute-start.2 = (f32[1,48,128]{2,1,0:T(8,128)S(1)}, f32[1,48,128]{2,1,0:T(8,128)S(1)}, u32[]{:S(2)}, u32[]{:S(2)}) collective-permute-start(f32[1,48,128]{2,1,0:T(8,128)S(1)} %maximum_bitcast_fusion), channel_id=1, source_target_pairs={{0,2},{1,3},{2,0},{3,1},{4,6},{5,7},{6,4},{7,5},{8,10},{9,11},{10,... | collective-permute-start | bytes 73736 | tf_op jit(solution)/shard_map/ppermute | solution.py:521
  12.8 100.6 %copy-start = (f32[2,768,8]{2,1,0:T(8,128)S(1)}, f32[2,768,8]{2,1,0:T(8,128)}, u32[]{:S(2)}) copy-start(f32[2,768,8]{2,1,0:T(8,128)} %copy.33.refs_16_.down) | copy-start | bytes 147460
  12.8 101.0 %copy-start.9 = (f32[2,8,768]{2,1,0:T(8,128)S(1)}, f32[2,8,768]{2,1,0:T(8,128)}, u32[]{:S(2)}) copy-start(f32[2,8,768]{2,1,0:T(8,128)} %refs_17_.1) | copy-start | bytes 147460
  112.1 25.0 %collective-permute-start.3 = (f32[104,128]{1,0:T(8,128)}, f32[104,128]{1,0:T(8,128)S(1)}, u32[]{:S(2)}, u32[]{:S(2)}) collective-permute-start(f32[104,128]{1,0:T(8,128)} %get-tuple-element.21), channel_id=1, source_target_pairs={{0,1},{1,0},{2,3},{3,2},{4,5},{5,4},{6,7},{7,6},{8,9},{9,8},{10,11... | collective-permute-start | bytes 159752 | tf_op jit(solution)/shard_map/ppermute | solution.py:616
  113.8 1.3 copy-start.1
  115.1 1.3 copy-start.2
  116.4 1.3 copy-start.3
  117.7 2.3 %copy-start.4 = (f32[1536,768]{1,0:T(8,128)S(1)}, f32[1536,768]{1,0:T(8,128)}, u32[]{:S(2)}) copy-start(f32[1536,768]{1,0:T(8,128)} %get-tuple-element.15.mg) | copy-start | bytes 14155780
  120.0 1.7 %copy-start.5 = (bf16[1536,768]{1,0:T(8,128)(2,1)S(1)}, bf16[1536,768]{1,0:T(8,128)(2,1)}, u32[]{:S(2)}) copy-start(bf16[1536,768]{1,0:T(8,128)(2,1)} %get-tuple-element.16.dq) | copy-start | bytes 7077892
  121.7 1.7 %copy-start.6 = (bf16[1536,768]{1,0:T(8,128)(2,1)S(1)}, bf16[1536,768]{1,0:T(8,128)(2,1)}, u32[]{:S(2)}) copy-start(bf16[1536,768]{1,0:T(8,128)(2,1)} %get-tuple-element.17.dk) | copy-start | bytes 7077892
  123.3 1.7 %copy-start.7 = (bf16[1536,768]{1,0:T(8,128)(2,1)S(1)}, bf16[1536,768]{1,0:T(8,128)(2,1)}, u32[]{:S(2)}) copy-start(bf16[1536,768]{1,0:T(8,128)(2,1)} %get-tuple-element.18.dv) | copy-start | bytes 7077892
  125.0 1.1 copy-start.8
  126.1 11.0 %copy-start.11 = (f32[3072]{0:T(1024)S(1)}, f32[3072]{0:T(1024)}, u32[]{:S(2)}) copy-start(f32[3072]{0:T(1024)} %param.42) | copy-start | bytes 36868
  126.1 11.0 %copy-start.12 = (f32[3072]{0:T(1024)S(1)}, f32[3072]{0:T(1024)}, u32[]{:S(2)}) copy-start(f32[3072]{0:T(1024)} %param.41) | copy-start | bytes 36868
  126.1 11.0 %copy-start.10 = (f32[104,128]{1,0:T(8,128)S(1)}, f32[104,128]{1,0:T(8,128)}, u32[]{:S(2)}) copy-start(f32[104,128]{1,0:T(8,128)} %get-tuple-element.20) | copy-start | bytes 159748
  137.2 3.5 %collective-permute-start.5 = (f32[104,128]{1,0:T(8,128)S(1)}, f32[104,128]{1,0:T(8,128)S(1)}, u32[]{:S(2)}, u32[]{:S(2)}) collective-permute-start(f32[104,128]{1,0:T(8,128)S(1)} %add.48), channel_id=1, source_target_pairs={{0,16},{8,24},{16,0},{24,8},{1,17},{9,25},{17,1},{25,9},{2,18},{10... | collective-permute-start | bytes 159752 | tf_op jit(solution)/shard_map/ppermute | solution.py:521
  138.7 3.9 %collective-permute-start.6 = (f32[104,128]{1,0:T(8,128)S(1)}, f32[104,128]{1,0:T(8,128)S(1)}, u32[]{:S(2)}, u32[]{:S(2)}) collective-permute-start(f32[104,128]{1,0:T(8,128)S(1)} %add.48), channel_id=1, source_target_pairs={{0,24},{8,16},{16,8},{24,0},{1,25},{9,17},{17,9},{25,1},{2,26},{10... | collective-permute-start | bytes 159752 | tf_op jit(solution)/shard_map/ppermute | solution.py:521
  139.9 3.3 %collective-permute-start.4 = (f32[104,128]{1,0:T(8,128)S(1)}, f32[104,128]{1,0:T(8,128)S(1)}, u32[]{:S(2)}, u32[]{:S(2)}) collective-permute-start(f32[104,128]{1,0:T(8,128)S(1)} %add.48), channel_id=1, source_target_pairs={{0,8},{8,0},{16,24},{24,16},{1,9},{9,1},{17,25},{25,17},{2,10},{10... | collective-permute-start | bytes 159752 | tf_op jit(solution)/shard_map/ppermute | solution.py:521
  143.2 3.9 %collective-permute-start.8 = (f32[104,128]{1,0:T(8,128)S(1)}, f32[104,128]{1,0:T(8,128)S(1)}, u32[]{:S(2)}, u32[]{:S(2)}) collective-permute-start(f32[104,128]{1,0:T(8,128)S(1)} %add_add_fusion.1), channel_id=1, source_target_pairs={{0,4},{1,5},{2,6},{3,7},{4,0},{5,1},{6,2},{7,3},{8,12},{9,13},{10,... | collective-permute-start | bytes 159752 | tf_op jit(solution)/shard_map/ppermute | solution.py:521
  145.3 5.1 %collective-permute-start.9 = (f32[104,128]{1,0:T(8,128)S(1)}, f32[104,128]{1,0:T(8,128)S(1)}, u32[]{:S(2)}, u32[]{:S(2)}) collective-permute-start(f32[104,128]{1,0:T(8,128)S(1)} %add_add_fusion.1), channel_id=1, source_target_pairs={{0,6},{1,7},{2,4},{3,5},{4,2},{5,3},{6,0},{7,1},{8,14},{9,15},{10,... | collective-permute-start | bytes 159752 | tf_op jit(solution)/shard_map/ppermute | solution.py:521
  146.8 3.6 %collective-permute-start.7 = (f32[104,128]{1,0:T(8,128)S(1)}, f32[104,128]{1,0:T(8,128)S(1)}, u32[]{:S(2)}, u32[]{:S(2)}) collective-permute-start(f32[104,128]{1,0:T(8,128)S(1)} %add_add_fusion.1), channel_id=1, source_target_pairs={{0,2},{1,3},{2,0},{3,1},{4,6},{5,7},{6,4},{7,5},{8,10},{9,11},{10,... | collective-permute-start | bytes 159752 | tf_op jit(solution)/shard_map/ppermute | solution.py:521
  151.7 3.6 %collective-permute-start.10 = (f32[96,128]{1,0:T(8,128)S(1)}, f32[96,128]{1,0:T(8,128)S(1)}, u32[]{:S(2)}, u32[]{:S(2)}) collective-permute-start(f32[96,128]{1,0:T(8,128)S(1)} %get-tuple-element.28), channel_id=1, source_target_pairs={{0,1},{1,0},{2,3},{3,2},{4,5},{5,4},{6,7},{7,6},{8,9},{9,8},{10,11... | collective-permute-start | bytes 147464 | tf_op jit(solution)/shard_map/ppermute | solution.py:652
where the time goes:
time: 158 us; the launch traced here: 157 us
  Pallas kernels  108 us (68%)
  local copies, waits for them, and re-layouts  22.7 us (14%)
  starting transfers between devices  15.1 us (10%)
  waiting for transfers between devices  6.88 us (4%)
  between operations  2.87 us (2%)
  other arithmetic  1.59 us (1%)
    pallas_call x1, Pallas kernels, layer(): pl.pallas_call(body, out_shape=out_shape, in_specs=in_specs, out_specs=[a...  99.3 us
    unnamed x28, local copies, waits for them, and re-layouts  15.1 us
    ppermute x9, starting transfers between devices, exchange(): lax.ppermute(values, axis, swap_perm(size, j << low))  11.1 us
    pallas_call x1, Pallas kernels, token_gradient(): pl.pallas_call(token_kernel, grid=(t // size,), out_shape=sds((t, d), bf1...  8.87 us
    ppermute x9, waiting for transfers between devices, exchange(): lax.ppermute(values, axis, swap_perm(size, j << low))  6.6 us
    reshape x4, local copies, waits for them, and re-layouts, per_device(): v.reshape(1, -1)  5.07 us
  transfers between devices with their start and end apart: 11, of which 6 were waited for; matrix products, arithmetic and copies ran while one was open for 5% of the time, Pallas kernels for 69%

commit v1 on v0

--- a/solution.py
+++ b/solution.py
@@ -56,6 +56,53 @@
 
 def row_mean(values):
     return jnp.sum(values, axis=1, keepdims=True) * (1.0 / values.shape[1])
+
+
+def lane_is_rank(rank):
+    shape = (rank, LANES)
+    return lax.broadcasted_iota(jnp.int32, shape, 1) % rank == lax.broadcasted_iota(
+        jnp.int32, shape, 0
+    )
+
+
+def lane_is_feature(rows, rank):
+    shape = (rows, LANES)
+    return lax.broadcasted_iota(jnp.int32, shape, 0) % (LANES // rank) == (
+        lax.broadcasted_iota(jnp.int32, shape, 1) // rank
+    )
+
+
+def flatten_pair(flat, j, spread, up, scale):
+    rank, width = up.shape
+    group = LANES // rank
+    down_rows = width // group
+    part = jnp.where(lane_is_feature(width, rank), spread, 0.0)
+    flat[j * down_rows : (j + 1) * down_rows, :] = jnp.sum(
+        part.reshape(down_rows, group, LANES), axis=1
+    )
+    up_rows = width // LANES
+    base = 2 * down_rows + j * rank * up_rows
+    for cb in range(up_rows):
+        flat[pl.ds(base + cb, rank, stride=up_rows), :] = (
+            scale * up[:, cb * LANES : (cb + 1) * LANES]
+        )
+
+
+def row_moves(wide, chunk_rows):
+    unit = 8 if chunk_rows % 8 == 0 else 1
+    for h in range(wide // 2):
+        for k in range(0, chunk_rows, unit):
+            yield h * chunk_rows + k, 2 * h * chunk_rows + k, unit
+
+
+def aligned(row, unit):
+    return pl.multiple_of(row, unit) if unit > 1 else row
+
+
+def split_half(flat, out, core, wide):
+    chunk_rows = flat.shape[0] // wide
+    for at, row, unit in row_moves(wide, chunk_rows):
+        out[at : at + unit, :] = flat[pl.ds(aligned(row + core * chunk_rows, unit), unit), :]
 
 
 def layer_kernel(
@@ -75,7 +122,7 @@
     b2,
     gains,
     shifts,
-    down,
+    down_t,
     up,
     mixed_hbm,
     midg_hbm,
@@ -85,6 +132,7 @@
     dg_hbm,
     keep_out,
     send_out,
+    params_out,
     x,
     cot,
     wq,
@@ -130,6 +178,7 @@
     n_pair = d_model // LANES
     ff = w1.shape[1]
     rank = up.shape[1]
+    core = lax.rem(lax.axis_index("wide"), 2)
 
     def bucket_copy(i, src, dst, sem):
         rows = pl.ds(i * BUCKET, BUCKET)
@@ -148,13 +197,8 @@
     for c in x_copies[1:] + cot_copies[1:]:
         c.start()
 
-    down_q = down[0].astype(bf16)
-    down_v = down[1].astype(bf16)
-    r_i = lax.broadcasted_iota(jnp.int32, (rank, LANES), 0)
-    l_i = lax.broadcasted_iota(jnp.int32, (rank, LANES), 1)
-    acat[...] = (
-        cdot(down_q, (l_i == r_i).astype(bf16), 1, 0)
-        + cdot(down_v, (l_i == r_i + rank).astype(bf16), 1, 0)
+    acat[...] = jnp.concatenate(
+        [down_t[0], down_t[1], jnp.zeros((LANES - 2 * rank, d_model), f32)], axis=0
     ).astype(bf16)
     up_q = up[0].astype(bf16).astype(f32) * adapter_scale
     up_v = up[1].astype(bf16).astype(f32) * adapter_scale
@@ -166,6 +210,10 @@
     ).astype(bf16)
     brep_q[...] = jnp.concatenate([up_q] * (LANES // rank), axis=0).astype(bf16)
     brep_v[...] = jnp.concatenate([up_v] * (LANES // rank), axis=0).astype(bf16)
+    for j in range(2):
+        spread = cdot(down_t[j], lane_is_rank(rank).astype(f32), 0, 0, lax.Precision.HIGHEST)
+        flatten_pair(flat, j, spread, up[j], 1.0)
+    split_half(flat, params_out, core, wide)
     seq = 0
     row0 = 0
     n_valid = 0
@@ -224,7 +272,7 @@
         size = 256
         lrows = pl.ds(pl.multiple_of(c * size, size), size)
         grows = pl.ds(pl.multiple_of(b * BUCKET + c * size, size), size)
-        ms = cdot(ctx[lrows, :], wo[...], 1, 0) + bo[...] + x[grows, :].astype(f32)
+        ms = cdot(ctx[lrows, :], wo[...], 1, 0) + bo[...][None] + x[grows, :].astype(f32)
         xc = ms - row_mean(ms)
         r1 = lax.rsqrt(row_mean(xc * xc) + norm_eps)
         n1 = xc * r1
@@ -232,12 +280,12 @@
         nl = normed.astype(bf16)
         step = 512
         for n in range(0, ff, step):
-            h = cdot(nl, w1[:, n : n + step], 1, 0) + b1[:, n : n + step]
+            h = cdot(nl, w1[:, n : n + step], 1, 0) + b1[n : n + step][None]
             cdf = 0.5 + 0.5 * lax.erf(h * (0.5**0.5))
             pdf = jnp.exp(h * h * -0.5) * 0.3989422804014327
             act[:, n : n + step] = (h * cdf).astype(bf16)
             slope[:, n : n + step] = (cdf + h * pdf).astype(bf16)
-        fs = cdot(act[...], w2[...], 1, 0) + b2[...] + normed
+        fs = cdot(act[...], w2[...], 1, 0) + b2[...][None] + normed
         fc = fs - row_mean(fs)
         r2 = lax.rsqrt(row_mean(fc * fc) + norm_eps)
         n2 = fc * r2
@@ -280,14 +328,14 @@
                 c.wait()
 
         xb = x[rows, :]
-        dnb = cdot(xb, acat[...], 1, 0).astype(bf16)
+        dnb = cdot(xb, acat[...], 1, 1).astype(bf16)
         dn[...] = dnb
         qs[...] = (
-            (cdot(xb, wq[...], 1, 0) + bq[...] + cdot(dnb, bcat_q[...], 1, 0)).astype(bf16)
+            (cdot(xb, wq[...], 1, 0) + bq[...][None] + cdot(dnb, bcat_q[...], 1, 0)).astype(bf16)
             * jnp.asarray(HEAD_DIM**-0.5, bf16)
         )
         ks[...] = cdot(xb, wk[...], 1, 0).astype(bf16)
-        vs[...] = (cdot(xb, wv[...], 1, 0) + bv[...] + cdot(dnb, bcat_v[...], 1, 0)).astype(bf16)
+        vs[...] = (cdot(xb, wv[...], 1, 0) + bv[...][None] + cdot(dnb, bcat_v[...], 1, 0)).astype(bf16)
 
         first = 0
         for i, length in enumerate((LEN_A, LEN_B, LEN_C)):
@@ -346,37 +394,17 @@
 
     lax.fori_loop(0, n_bucket, bucket, 0)
 
-    group = LANES // rank
-    half_rows = d_model // group
-    up_rows = d_model // LANES
-    row_i = lax.broadcasted_iota(jnp.int32, (d_model, LANES), 0)
-    lane_i = lax.broadcasted_iota(jnp.int32, (d_model, LANES), 1)
-    pick = (row_i % group) == (lane_i // rank)
-    for j in range(2):
-        part = jnp.where(pick, g_down[:, j * LANES : (j + 1) * LANES], 0.0)
-        flat[j * half_rows : (j + 1) * half_rows, :] = jnp.sum(
-            part.reshape(half_rows, group, LANES), axis=1
+    for j, src in enumerate((g_up_q, g_up_v)):
+        flatten_pair(
+            flat,
+            j,
+            g_down[:, j * LANES : (j + 1) * LANES],
+            src[j * rank : (j + 1) * rank, :],
+            adapter_scale,
         )
-        src = (g_up_q, g_up_v)[j]
-        base = 2 * half_rows + j * rank * up_rows
-        for cb in range(up_rows):
-            flat[pl.ds(base + cb, rank, stride=up_rows), :] = adapter_scale * (
-                src[j * rank : (j + 1) * rank, cb * LANES : (cb + 1) * LANES]
-            )
-    core = lax.rem(lax.axis_index("wide"), 2)
     n_rows = flat.shape[0]
-    chunk_rows = n_rows // wide
-    unit = 8 if chunk_rows % 8 == 0 else 1
-    for h in range(wide // 2):
-        for k in range(0, chunk_rows, unit):
-            at = h * chunk_rows + k
-            mine = 2 * h * chunk_rows + k + core * chunk_rows
-            other = 2 * h * chunk_rows + k + (1 - core) * chunk_rows
-            if unit == 8:
-                mine = pl.multiple_of(mine, 8)
-                other = pl.multiple_of(other, 8)
-            keep_out[at : at + unit, :] = flat[pl.ds(mine, unit), :]
-            send_out[at : at + unit, :] = flat[pl.ds(other, unit), :]
+    split_half(flat, keep_out, core, wide)
+    split_half(flat, send_out, 1 - core, wide)
     total = jnp.full((8, LANES), n_valid, jnp.int32).astype(f32)
     keep_out[n_rows // 2 :, :] = total
     send_out[n_rows // 2 :, :] = total
@@ -385,15 +413,15 @@
             bucket_copy(j, src, dst, out_sem.at[i * n_bucket + j]).wait()
 
 
-def layer(lens, x, cot, ws, vecs, gains, shifts, down, up, wide):
+def layer(lens, x, cot, ws, vecs, gains, shifts, down_t, up, wide):
     t, d = x.shape
     ff = ws[4].shape[1]
     rank = up.shape[1]
-    n_rows = 2 * down.size // LANES
+    n_rows = 2 * down_t.size // LANES
     n_bucket = t // BUCKET
     any_spec = pl.BlockSpec(memory_space=pl.ANY)
     vm = pl.BlockSpec(memory_space=VMEM)
-    ops = [lens, x, cot, *ws, *vecs, gains, shifts, down, up]
+    ops = [lens, x, cot, *ws, *vecs, gains, shifts, down_t, up]
     in_specs = (
         [pl.BlockSpec(memory_space=pltpu.SMEM)] + [any_spec] * 8 + [vm] * (len(vecs) + 4)
     )
@@ -406,6 +434,7 @@
         sds((t, 2 * LANES), bf16),
         sds((n_rows // 2 + 8, LANES), f32),
         sds((n_rows // 2 + 8, LANES), f32),
+        sds((n_rows // 2, LANES), f32),
     ]
     dma = pltpu.SemaphoreType.DMA
     scratch = [
@@ -417,7 +446,7 @@
         VMEM((d, d), bf16),
         VMEM((d, ff), bf16),
         VMEM((ff, d), bf16),
-        VMEM((d, LANES), bf16),
+        VMEM((LANES, d), bf16),
         VMEM((LANES, d), bf16),
         VMEM((LANES, d), bf16),
         VMEM((LANES, d), bf16),
@@ -452,52 +481,162 @@
         body,
         out_shape=out_shape,
         in_specs=in_specs,
-        out_specs=[any_spec] * 6 + [vm] * 2,
+        out_specs=[any_spec] * 6 + [vm] * 3,
         scratch_shapes=scratch,
         compiler_params=pltpu.CompilerParams(vmem_limit_bytes=63 << 20),
         name="layer",
     )(*ops)
 
 
-def token_kernel(mg, dq, dk, dv, dg, wq, wk, wv, down, out):
-    down_q = down[0].astype(bf16)
-    down_v = down[1].astype(bf16)
+def token_kernel(prev, after, mg, dq, dk, dv, dg, wq, wk, wv, down_t, out):
+    width = wq.shape[0]
+    fill = jnp.zeros((LANES - down_t.shape[1], width), f32)
+    down = jnp.concatenate([down_t[0], fill, down_t[1], fill], axis=0).astype(bf16)
     acc = mg[...] + cdot(dq[...], wq[...], 1, 1)
     acc = acc + cdot(dk[...], wk[...], 1, 1)
     acc = acc + cdot(dv[...], wv[...], 1, 1)
-    rank = down.shape[2]
-    acc = acc + cdot(dg[:, :rank], down_q, 1, 1)
-    acc = acc + cdot(dg[:, LANES : LANES + rank], down_v, 1, 1)
+    acc = acc + cdot(dg[...], down, 1, 0)
     out[...] = acc.astype(bf16)
 
 
-def token_gradient(mg, dq, dk, dv, dg, wq, wk, wv, down):
+def token_gradient(prev, after, mg, dq, dk, dv, dg, wq, wk, wv, down_t, part, parts):
     t, d = mg.shape
     size = 256
-    row = lambda i: (i, 0)
+    steps = t // size // parts
+    row = lambda i: (i + part * steps, 0)
     fixed = lambda i: (0, 0)
+    any_spec = pl.BlockSpec(memory_space=pl.ANY)
+    args = (after, mg, dq, dk, dv, dg, wq, wk, wv, down_t)
+    specs = [
+        any_spec,
+        pl.BlockSpec((size, d), row),
+        pl.BlockSpec((size, d), row),
+        pl.BlockSpec((size, d), row),
+        pl.BlockSpec((size, d), row),
+        pl.BlockSpec((size, 2 * LANES), row),
+        pl.BlockSpec((d, d), fixed),
+        pl.BlockSpec((d, d), fixed),
+        pl.BlockSpec((d, d), fixed),
+        pl.BlockSpec(down_t.shape, lambda i: (0, 0, 0)),
+    ]
+    if prev is None:
+        body = lambda *refs: token_kernel(None, *refs)
+        aliases = {}
+    else:
+        body = token_kernel
+        args = (prev,) + args
+        specs = [any_spec] + specs
+        aliases = {0: 0}
     return pl.pallas_call(
-        token_kernel,
-        grid=(t // size,),
+        body,
+        grid=(steps,),
         out_shape=sds((t, d), bf16),
-        in_specs=[
-            pl.BlockSpec((size, d), row),
-            pl.BlockSpec((size, d), row),
-            pl.BlockSpec((size, d), row),
-            pl.BlockSpec((size, d), row),
-            pl.BlockSpec((size, 2 * LANES), row),
-            pl.BlockSpec((d, d), fixed),
-            pl.BlockSpec((d, d), fixed),
-            pl.BlockSpec((d, d), fixed),
-            pl.BlockSpec(down.shape, lambda i: (0, 0, 0)),
-        ],
+        in_specs=specs,
         out_specs=pl.BlockSpec((size, d), row),
-        compiler_params=pltpu.CompilerParams(vmem_limit_bytes=24 << 20),
+        input_output_aliases=aliases,
+        compiler_params=pltpu.CompilerParams(vmem_limit_bytes=60 << 20),
         cost_estimate=pl.CostEstimate(
-            flops=6 * t * d * d, bytes_accessed=14 * t * d, transcendentals=0
+            flops=6 * t * d * d // parts, bytes_accessed=14 * t * d // parts, transcendentals=0
         ),
         name="token_gradient",
-    )(mg, dq, dk, dv, dg, wq, wk, wv, down)
+    )(*args)
+
+
+def adam_kernel(beta_one, beta_two, step, *refs, n, held, wide, low):
+    pieces = refs[:n]
+    params, new_params, first_out, second_out, first, second, new_first, new_second = refs[n:]
+    rows = params.shape[0]
+    chunk_rows = 2 * rows // wide
+    place = lax.axis_index("wide")
+    digit = (place >> low) % n
+    block = held * chunk_rows
+    unit = 8 if block % 8 == 0 else 1
+    for j, piece in enumerate(pieces):
+        at = aligned((digit ^ j) * block, unit)
+        first[pl.ds(at, block), :] = piece[rows + 8 : rows + 8 + block, :]
+        second[pl.ds(at, block), :] = piece[rows + 8 + block : rows + 8 + 2 * block, :]
+    total = tree_sum([p[: rows + 8, :] for p in pieces])
+    gradient = total[:rows] / total[rows : rows + 1]
+    b1 = jnp.full((8, LANES), beta_one[0], f32)
+    b2 = jnp.full((8, LANES), beta_two[0], f32)
+    count = step[0]
+    power1 = jnp.ones((8, LANES), f32)
+    power2 = power1
+    square1, square2 = b1, b2
+    for bit in range(16):
+        on = ((count >> bit) & 1) == 1
+        power1 = jnp.where(on, power1 * square1, power1)
+        power2 = jnp.where(on, power2 * square2, power2)
+        square1 = square1 * square1
+        square2 = square2 * square2
+    b1, b2 = b1[:1], b2[:1]
+    m = b1 * first[...] + (1.0 - b1) * gradient
+    v = b2 * second[...] + (1.0 - b2) * gradient * gradient
+    inside_first = lax.broadcasted_iota(jnp.int32, (rows, LANES), 0) < rows // 2
+    rate = jnp.where(inside_first, rate_first, rate_second)
+    decay = jnp.where(inside_first, decay_first, decay_second)
+    new_params[...] = params[...] * (1.0 - rate * decay) - rate * (m / (1.0 - power1[:1])) / (
+        jnp.sqrt(v / (1.0 - power2[:1])) + adam_eps
+    )
+    new_first[...] = m
+    new_second[...] = v
+    own = (place // 2) * chunk_rows
+    unit = 8 if chunk_rows % 8 == 0 else 1
+    for k in range(0, chunk_rows, unit):
+        at = aligned(own + k, unit)
+        first_out[k : k + unit, :] = new_first[pl.ds(at, unit), :]
+        second_out[k : k + unit, :] = new_second[pl.ds(at, unit), :]
+
+
+def adam(beta_one, beta_two, step, pieces, params, held, wide, low):
+    rows = params.shape[0]
+    chunk_rows = 2 * rows // wide
+    smem = pl.BlockSpec(memory_space=pltpu.SMEM)
+    vm = pl.BlockSpec(memory_space=VMEM)
+    n = len(pieces)
+    return pl.pallas_call(
+        lambda *refs: adam_kernel(*refs, n=n, held=held, wide=wide, low=low),
+        out_shape=[sds((rows, LANES), f32)] + [sds((chunk_rows, LANES), f32)] * 2,
+        in_specs=[smem] * 3 + [vm] * (n + 1),
+        out_specs=[vm] * 3,
+        scratch_shapes=[VMEM((rows, LANES), f32)] * 4,
+        name="adam",
+    )(beta_one, beta_two, step, *pieces, params)
+
+
+def unflatten_kernel(own, other, down_t, up, flat, *, wide):
+    core = lax.rem(lax.axis_index("wide"), 2)
+    rank, width = up.shape[1:]
+    chunk_rows = flat.shape[0] // wide
+    for at, row, unit in row_moves(wide, chunk_rows):
+        flat[pl.ds(aligned(row + core * chunk_rows, unit), unit), :] = own[at : at + unit, :]
+        flat[pl.ds(aligned(row + (1 - core) * chunk_rows, unit), unit), :] = other[
+            at : at + unit, :
+        ]
+    group = LANES // rank
+    down_rows = width // group
+    up_rows = width // LANES
+    for j in range(2):
+        spread = jnp.broadcast_to(
+            flat[j * down_rows : (j + 1) * down_rows, :][:, None, :], (down_rows, group, LANES)
+        ).reshape(width, LANES)
+        part = jnp.where(lane_is_feature(width, rank), spread, 0.0)
+        down_t[j] = cdot(lane_is_rank(rank).astype(f32), part, 1, 1, lax.Precision.HIGHEST)
+        base = 2 * down_rows + j * rank * up_rows
+        for cb in range(up_rows):
+            up[j, :, cb * LANES : (cb + 1) * LANES] = flat[pl.ds(base + cb, rank, stride=up_rows), :]
+
+
+def unflatten(own, other, down_shape, up_shape, wide):
+    vm = pl.BlockSpec(memory_space=VMEM)
+    return pl.pallas_call(
+        lambda *refs: unflatten_kernel(*refs, wide=wide),
+        out_shape=[sds(down_shape, f32), sds(up_shape, f32)],
+        in_specs=[vm] * 2,
+        out_specs=[vm] * 2,
+        scratch_shapes=[VMEM((2 * own.shape[0], LANES), f32)],
+        name="unflatten",
+    )(own, other)
 
 
 def digit_groups(size, first):
@@ -565,26 +704,11 @@
     dp = lax.axis_size("dp")
     wide = lax.axis_size("wide")
     place = lax.axis_index("wide")
-    core = place % 2
     n_rows = 2 * adapter_down_factors.size // LANES
     chunk_rows = n_rows // wide
 
-    moments = jnp.concatenate(
-        [first_moment_estimate.reshape(chunk_rows, LANES), second_moment_estimate.reshape(chunk_rows, LANES)],
-        axis=0,
-    )[None]
-    for low, n in digit_groups(wide, 1):
-        parts = exchange(moments, "wide", wide, (low, n))
-        moments = jnp.concatenate(in_order(parts, place >> low), axis=0)
-    first_half = moments[:, :chunk_rows].reshape(n_rows // 2, LANES)
-    second_half = moments[:, chunk_rows:].reshape(n_rows // 2, LANES)
-
-    params = jnp.concatenate(
-        [adapter_down_factors.reshape(-1), adapter_up_factors.reshape(-1)]
-    ).reshape(wide // 2, 2, chunk_rows, LANES)
-    own_params = lax.dynamic_index_in_dim(params, core, 1, keepdims=False).reshape(n_rows // 2, LANES)
-
-    mixed, midg, dq, dk, dv, dg, keep, send = layer(
+    down_t = jnp.swapaxes(adapter_down_factors, 1, 2)
+    mixed, midg, dq, dk, dv, dg, keep, send, own_params = layer(
         valid_token_length,
         tokens,
         cotangent,
@@ -596,67 +720,79 @@
             inner_ffn_weight,
             outer_ffn_weight,
         ),
-        tuple(
-            v.reshape(1, -1)
-            for v in (
-                query_bias_vector,
-                value_bias_vector,
-                attention_output_bias,
-                hidden_ffn_bias,
-                ffn_output_bias,
-            )
+        (
+            query_bias_vector,
+            value_bias_vector,
+            attention_output_bias,
+            hidden_ffn_bias,
+            ffn_output_bias,
         ),
         layer_norm_gains,
         layer_norm_biases,
-        adapter_down_factors,
+        down_t,
         adapter_up_factors,
         wide,
     )
 
+    def token_part(prev, after, part):
+        return token_gradient(
+            prev,
+            after,
+            midg,
+            dq,
+            dk,
+            dv,
+            dg,
+            query_weight_matrix,
+            key_weight_matrix,
+            value_weight_matrix,
+            down_t,
+            part,
+            2,
+        )
+
     grad = keep + lax.ppermute(send, "wide", swap_perm(wide, 1))
+    token_grad = token_part(None, grad, 0)
     for group in digit_groups(dp, 0):
         grad = tree_sum(exchange(grad, "dp", dp, group))
-    for group in digit_groups(wide, 1):
-        grad = tree_sum(exchange(grad, "wide", wide, group))
-
-    input_token_gradient = token_gradient(
-        midg,
-        dq,
-        dk,
-        dv,
-        dg,
-        query_weight_matrix,
-        key_weight_matrix,
-        value_weight_matrix,
-        adapter_down_factors,
-    )
-
-    count = grad[n_rows // 2, 0]
-    gradient = grad[: n_rows // 2] / count
-    beta_one = first_decay_factor[0]
-    beta_two = second_decay_factor[0]
-    step = optimizer_step_number[0].astype(f32)
-    inside_first = lax.broadcasted_iota(jnp.int32, (n_rows // 2, LANES), 0) < n_rows // 4
-    step_rate = jnp.where(inside_first, rate_first, rate_second)
-    decay_rate = jnp.where(inside_first, decay_first, decay_second)
-    new_first = beta_one * first_half + (1.0 - beta_one) * gradient
-    new_second = beta_two * second_half + (1.0 - beta_two) * gradient * gradient
-    first_hat = new_first / (1.0 - jnp.power(beta_one, step))
-    second_hat = new_second / (1.0 - jnp.power(beta_two, step))
-    new_params = own_params * (1.0 - step_rate * decay_rate) - step_rate * first_hat / (
-        jnp.sqrt(second_hat) + adam_eps
-    )
-    own = (place // 2) * chunk_rows
-    updated_first = lax.dynamic_slice_in_dim(new_first, own, chunk_rows, 0).reshape(-1)
-    updated_second = lax.dynamic_slice_in_dim(new_second, own, chunk_rows, 0).reshape(-1)
+    token_grad = token_part(token_grad, grad, 1)
+
+    first = first_moment_estimate.reshape(chunk_rows, LANES)
+    second = second_moment_estimate.reshape(chunk_rows, LANES)
+    held = 1
+    rows = n_rows // 2 + 8
+    groups = digit_groups(wide, 1)
+    for i, (low, n) in enumerate(groups):
+        pieces = exchange(jnp.concatenate([grad, first, second], axis=0), "wide", wide, (low, n))
+        if i + 1 < len(groups):
+            grad = tree_sum([p[:rows] for p in pieces])
+            block = held * chunk_rows
+            pieces = in_order(pieces, place >> low)
+            first = jnp.concatenate([p[rows : rows + block] for p in pieces], axis=0)
+            second = jnp.concatenate([p[rows + block :] for p in pieces], axis=0)
+            held *= len(pieces)
+    new_params, updated_first, updated_second = adam(
+        first_decay_factor,
+        second_decay_factor,
+        optimizer_step_number,
+        pieces,
+        own_params,
+        held,
+        wide,
+        groups[-1][0],
+    )
     other_params = lax.ppermute(new_params, "wide", swap_perm(wide, 1))
-    halves = [
-        v.reshape(wide // 2, 1, chunk_rows, LANES) for v in in_order([new_params, other_params], core)
-    ]
-    whole = jnp.concatenate(halves, axis=1).reshape(-1)
-    updated_down = whole[: adapter_down_factors.size].reshape(adapter_down_factors.shape)
-    updated_up = whole[adapter_down_factors.size :].reshape(adapter_up_factors.shape)
-    return (mixed, input_token_gradient, updated_down, updated_up, updated_first, updated_second)
+    updated_down_t, updated_up = unflatten(
+        new_params, other_params, down_t.shape, adapter_up_factors.shape, wide
+    )
+    return (
+        mixed,
+        token_grad,
+        jnp.swapaxes(updated_down_t, 1, 2),
+        updated_up,
+        updated_first.reshape(-1),
+        updated_second.reshape(-1),
+    )
 
 
 def solution(mesh):

time: 158 us -> 137 us (0.87)
  local copies, waits for them, and re-layouts: 22.7 us -> 1.29 us
  Pallas kernels: 108 us -> 119 us
  starting transfers between devices: 15.1 us -> 10.3 us
  waiting for transfers between devices: 6.88 us -> 2.35 us
    unnamed x28 -> x18, local copies, waits for them, and re-layouts: 15.1 us -> 1.29 us
    pallas_call x1 -> x4, Pallas kernels: 8.87 us -> 19.3 us  [the longest x2 15.4 us: token_gradient(): pl.pallas_call(body, grid=(steps,), out_shape=sds((t, d), bf16), in_specs...]
    reshape x7 -> x0, local copies, waits for them, and re-layouts: 6.73 us -> none  [the longest x4 5.07 us: per_device(): v.reshape(1, -1)]
    ppermute x9 -> x6, waiting for transfers between devices: 6.6 us -> 0.95 us  [exchange(): lax.ppermute(values, axis, swap_perm(size, j << low))]
    ppermute x9 -> x6, starting transfers between devices: 11.1 us -> 8.12 us  [exchange(): lax.ppermute(values, axis, swap_perm(size, j << low))]
  transfers between devices with their start and end apart: 11 -> 8, of which waited for: 6 -> 3; matrix products, arithmetic and copies ran while one was open for 5% -> 0% of each run, Pallas kernels for 69% -> 11%
where the time goes in v1:
time: 137 us
  Pallas kernels  119 us (87%)
  starting transfers between devices  10.3 us (8%)
  between operations  2.73 us (2%)
  waiting for transfers between devices  2.35 us (2%)
    pallas_call x1, Pallas kernels, layer(): pl.pallas_call(body, out_shape=out_shape, in_specs=in_specs, out_specs=[a...  99.6 us
    pallas_call x2, Pallas kernels, token_gradient(): pl.pallas_call(body, grid=(steps,), out_shape=sds((t, d), bf16), in_specs...  15.4 us
    ppermute x6, starting transfers between devices, exchange(): lax.ppermute(values, axis, swap_perm(size, j << low))  8.12 us
  transfers between devices with their start and end apart: 8, of which 3 were waited for; matrix products, arithmetic and copies ran while one was open for 0% of the time, Pallas kernels for 11%

profile of v1, /device:TPU:1, one launch (start us, length us, event | category | flops | bytes accessed | tf_op | source)
XLA Modules:
  0.0 136.5 jit_solution(6867793972656114496)
XLA Ops:
  0.7 99.6 %layer.1 = (bf16[1536,768]{1,0:T(8,128)(2,1)}, f32[1536,768]{1,0:T(8,128)}, bf16[1536,768]{1,0:T(8,128)(2,1)}, bf16[1536,768]{1,0:T(8,128)(2,1)}, bf16[1536,768]...) custom-call(s32[7]{0:T(128)} %refs_0_.2, ...), custom_call_target="tpu_custom_call" | custom-call | tf_op jit(solution)/shard_map/layer/pallas_call | solution.py:480
  100.3 0.1 collective-permute-start
  100.4 1.4 %collective-permute-done = f32[104,128]{1,0:T(8,128)S(1)} collective-permute-done((f32[104,128]{1,0:T(8,128)}, f32[104,128]{1,0:T(8,128)S(1)}, u32[]{:S(2)}, u32[]{:S(2)}) %collective-permute-start) | collective-permute-done | bytes 53280 | tf_op jit(solution)/shard_map/ppermute | solution.py:754
  101.8 0.8 add.12.refs_0_
  102.6 2.5 %collective-permute-start.2 = (f32[104,128]{1,0:T(8,128)S(1)}, f32[104,128]{1,0:T(8,128)S(1)}, u32[]{:S(2)}, u32[]{:S(2)}) collective-permute-start(f32[104,128]{1,0:T(8,128)S(1)} %add.12.refs_0_), channel_id=1, source_target_pairs={{0,16},{8,24},{16,0},{24,8},{1,17},{9,25},{17,1},{25,9},{2,18},{10... | collective-permute-start | bytes 159752 | tf_op jit(solution)/shard_map/ppermute | solution.py:660
  105.1 1.2 collective-permute-start.3
  106.2 0.1 collective-permute-start.1
  108.3 0.0 collective-permute-done.2
  108.3 0.7 collective-permute-done.3
  109.0 0.3 collective-permute-done.1
  109.3 2.1 %collective-permute-start.4 = (f32[152,128]{1,0:T(8,128)S(1)}, f32[152,128]{1,0:T(8,128)S(1)}, u32[]{:S(2)}, u32[]{:S(2)}) collective-permute-start(f32[152,128]{1,0:T(8,128)S(1)} %pad_maximum_fusion.refs_3_), channel_id=1, source_target_pairs={{0,2},{1,3},{2,0},{3,1},{4,6},{5,7},{6,4},{7,5},{8,10},{9,11},{10,... | collective-permute-start | bytes 233480 | tf_op jit(solution)/shard_map/ppermute | solution.py:660
  111.4 2.3 %collective-permute-start.5 = (f32[152,128]{1,0:T(8,128)S(1)}, f32[152,128]{1,0:T(8,128)S(1)}, u32[]{:S(2)}, u32[]{:S(2)}) collective-permute-start(f32[152,128]{1,0:T(8,128)S(1)} %pad_maximum_fusion.refs_3_), channel_id=1, source_target_pairs={{0,4},{1,5},{2,6},{3,7},{4,0},{5,1},{6,2},{7,3},{8,12},{9,13},{10,... | collective-permute-start | bytes 233480 | tf_op jit(solution)/shard_map/ppermute | solution.py:660
  113.7 0.0 collective-permute-start.6
  113.7 7.7 %token_gradient.2.prev = bf16[1536,768]{1,0:T(8,128)(2,1)} custom-call(f32[104,128]{1,0:T(8,128)} %copy-done, f32[1536,768]{1,0:T(8,128)} %get-tuple-element.23.refs_1_.mg, bf16[1536,768]{1,0:T(8,128)(2,1)} %get-tuple-element.24.refs_2_.dq, bf16[1536,768]{1,0:T(8,128)(2,1)} %get-tuple-element.25.refs_3_.dk, bf16[1536,768]{1,0:T(8,128)(2,1)} %get-tuple-element.26.refs_4_.dv, ...), custom_call_target="tpu_custom_call" | custom-call | flops 2717908992 | bytes 8257536 | tf_op jit(solution)/shard_map/token_gradient/pallas_call | solution.py:530
  121.5 0.0 collective-permute-done.4.refs_4_
  121.5 0.0 collective-permute-done.5.refs_5_
  121.5 0.6 copy-done.3
  122.1 0.0 copy-done.4
  122.1 0.0 copy-done.5
  122.2 1.7 %adam.1 = (f32[96,128]{1,0:T(8,128)}, f32[24,128]{1,0:T(8,128)}, f32[24,128]{1,0:T(8,128)}) custom-call(f32[1]{0:T(128)S(6)} %copy.31.refs_0_, f32[1]{0:T(128)S(6)} %copy.32.refs_1_, s32[1]{0:T(128)S(6)} %copy.33.refs_2_, f32[152,128]{1,0:T(8,128)} %copy-done.2, f32[152,128]{1,0:T(8,128)} %copy-done.3, f32[152,128]{1,0:T(8,128)} %copy-done.4, ...), custom_call_target="tpu_custom_call" | custom-call | tf_op jit(solution)/shard_map/adam/pallas_call | solution.py:597
  123.9 2.1 %collective-permute-start.7 = (f32[96,128]{1,0:T(8,128)}, f32[96,128]{1,0:T(8,128)S(1)}, u32[]{:S(2)}, u32[]{:S(2)}) collective-permute-start(f32[96,128]{1,0:T(8,128)} %get-tuple-element.29.refs_0_), channel_id=1, source_target_pairs={{0,1},{1,0},{2,3},{3,2},{4,5},{5,4},{6,7},{7,6},{8,9},{9,8},{10,11... | collective-permute-start | bytes 147464 | tf_op jit(solution)/shard_map/ppermute | solution.py:784
  126.0 7.7 %token_gradient.3 = bf16[1536,768]{1,0:T(8,128)(2,1)} custom-call(bf16[1536,768]{1,0:T(8,128)(2,1)} %token_gradient.2.prev, f32[104,128]{1,0:T(8,128)} %copy-done.1, f32[1536,768]{1,0:T(8,128)} %get-tuple-element.23.refs_1_.mg, bf16[1536,768]{1,0:T(8,128)(2,1)} %get-tuple-element.24.refs_2_.dq, ...), custom_call_target="tpu_custom_call", output_to_operand_aliasing={{}: (0, {})} | custom-call | flops 2717908992 | bytes 8257536 | tf_op jit(solution)/shard_map/token_gradient/pallas_call | solution.py:530
  133.7 0.6 copy-done.6
  134.3 2.2 %unflatten.1 = (f32[2,8,768]{2,1,0:T(8,128)}, f32[2,8,768]{2,1,0:T(8,128)}) custom-call(f32[96,128]{1,0:T(8,128)} %get-tuple-element.29.refs_0_, f32[96,128]{1,0:T(8,128)} %copy-done.6), custom_call_target="tpu_custom_call" | custom-call | tf_op jit(solution)/shard_map/unflatten/pallas_call | solution.py:632
  (18 shorter events, 0.1 us)
Async XLA Ops:
  0.6 108.6 %copy-start.7 = (f32[3072]{0:T(1024)S(1)}, f32[3072]{0:T(1024)}, u32[]{:S(2)}) copy-start(f32[3072]{0:T(1024)} %param.42) | copy-start | bytes 36868
  0.6 108.6 %copy-start.8 = (f32[3072]{0:T(1024)S(1)}, f32[3072]{0:T(1024)}, u32[]{:S(2)}) copy-start(f32[3072]{0:T(1024)} %param.41) | copy-start | bytes 36868
  100.3 1.5 %collective-permute-start = (f32[104,128]{1,0:T(8,128)}, f32[104,128]{1,0:T(8,128)S(1)}, u32[]{:S(2)}, u32[]{:S(2)}) collective-permute-start(f32[104,128]{1,0:T(8,128)} %get-tuple-element.22), channel_id=1, source_target_pairs={{0,1},{1,0},{2,3},{3,2},{4,5},{5,4},{6,7},{7,6},{8,9},{9,8},{10,11... | collective-permute-start | bytes 159752 | tf_op jit(solution)/shard_map/ppermute | solution.py:754
  102.6 11.1 %copy-start = (f32[104,128]{1,0:T(8,128)}, f32[104,128]{1,0:T(8,128)S(1)}, u32[]{:S(2)}) copy-start(f32[104,128]{1,0:T(8,128)S(1)} %add.12.refs_0_) | copy-start | bytes 159748
  102.6 5.7 %collective-permute-start.2 = (f32[104,128]{1,0:T(8,128)S(1)}, f32[104,128]{1,0:T(8,128)S(1)}, u32[]{:S(2)}, u32[]{:S(2)}) collective-permute-start(f32[104,128]{1,0:T(8,128)S(1)} %add.12.refs_0_), channel_id=1, source_target_pairs={{0,16},{8,24},{16,0},{24,8},{1,17},{9,25},{17,1},{25,9},{2,18},{10... | collective-permute-start | bytes 159752 | tf_op jit(solution)/shard_map/ppermute | solution.py:660
  105.1 3.9 %collective-permute-start.3 = (f32[104,128]{1,0:T(8,128)S(1)}, f32[104,128]{1,0:T(8,128)S(1)}, u32[]{:S(2)}, u32[]{:S(2)}) collective-permute-start(f32[104,128]{1,0:T(8,128)S(1)} %add.12.refs_0_), channel_id=1, source_target_pairs={{0,24},{8,16},{16,8},{24,0},{1,25},{9,17},{17,9},{25,1},{2,26},{10... | collective-permute-start | bytes 159752 | tf_op jit(solution)/shard_map/ppermute | solution.py:660
  106.2 3.0 %collective-permute-start.1 = (f32[104,128]{1,0:T(8,128)S(1)}, f32[104,128]{1,0:T(8,128)S(1)}, u32[]{:S(2)}, u32[]{:S(2)}) collective-permute-start(f32[104,128]{1,0:T(8,128)S(1)} %add.12.refs_0_), channel_id=1, source_target_pairs={{0,8},{8,0},{16,24},{24,16},{1,9},{9,1},{17,25},{25,17},{2,10},{10... | collective-permute-start | bytes 159752 | tf_op jit(solution)/shard_map/ppermute | solution.py:660
  109.3 12.2 %copy-start.1 = (f32[104,128]{1,0:T(8,128)}, f32[104,128]{1,0:T(8,128)S(1)}, u32[]{:S(2)}) copy-start(f32[104,128]{1,0:T(8,128)S(1)} %add_add_fusion.after) | copy-start | bytes 159748
  109.3 12.1 %copy-start.2 = (f32[152,128]{1,0:T(8,128)}, f32[152,128]{1,0:T(8,128)S(1)}, u32[]{:S(2)}) copy-start(f32[152,128]{1,0:T(8,128)S(1)} %pad_maximum_fusion.refs_3_) | copy-start | bytes 233476
  109.3 12.1 %collective-permute-start.4 = (f32[152,128]{1,0:T(8,128)S(1)}, f32[152,128]{1,0:T(8,128)S(1)}, u32[]{:S(2)}, u32[]{:S(2)}) collective-permute-start(f32[152,128]{1,0:T(8,128)S(1)} %pad_maximum_fusion.refs_3_), channel_id=1, source_target_pairs={{0,2},{1,3},{2,0},{3,1},{4,6},{5,7},{6,4},{7,5},{8,10},{9,11},{10,... | collective-permute-start | bytes 233480 | tf_op jit(solution)/shard_map/ppermute | solution.py:660
  111.4 10.1 %collective-permute-start.5 = (f32[152,128]{1,0:T(8,128)S(1)}, f32[152,128]{1,0:T(8,128)S(1)}, u32[]{:S(2)}, u32[]{:S(2)}) collective-permute-start(f32[152,128]{1,0:T(8,128)S(1)} %pad_maximum_fusion.refs_3_), channel_id=1, source_target_pairs={{0,4},{1,5},{2,6},{3,7},{4,0},{5,1},{6,2},{7,3},{8,12},{9,13},{10,... | collective-permute-start | bytes 233480 | tf_op jit(solution)/shard_map/ppermute | solution.py:660
  113.7 7.8 %collective-permute-start.6 = (f32[152,128]{1,0:T(8,128)S(1)}, f32[152,128]{1,0:T(8,128)S(1)}, u32[]{:S(2)}, u32[]{:S(2)}) collective-permute-start(f32[152,128]{1,0:T(8,128)S(1)} %pad_maximum_fusion.refs_3_), channel_id=1, source_target_pairs={{0,6},{1,7},{2,4},{3,5},{4,2},{5,3},{6,0},{7,1},{8,14},{9,15},{10,... | collective-permute-start | bytes 233480 | tf_op jit(solution)/shard_map/ppermute | solution.py:660
  121.5 0.6 copy-start.3
  121.5 0.6 copy-start.4
  121.5 0.7 copy-start.5
  123.9 9.8 %collective-permute-start.7 = (f32[96,128]{1,0:T(8,128)}, f32[96,128]{1,0:T(8,128)S(1)}, u32[]{:S(2)}, u32[]{:S(2)}) collective-permute-start(f32[96,128]{1,0:T(8,128)} %get-tuple-element.29.refs_0_), channel_id=1, source_target_pairs={{0,1},{1,0},{2,3},{3,2},{4,5},{5,4},{6,7},{7,6},{8,9},{9,8},{10,11... | collective-permute-start | bytes 147464 | tf_op jit(solution)/shard_map/ppermute | solution.py:784
  133.7 0.6 copy-start.6

commit v2 on v1

v2 whole, which is shorter than its diff:
```python
import jax
import jax.numpy as jnp
from jax import lax
from jax.experimental import pallas as pl
from jax.experimental.pallas import tpu as pltpu
from jax.sharding import PartitionSpec as P

HEADS = 12
HEAD_DIM = 64
LEN_A = 128
LEN_B = 256
LEN_C = 512
BUCKET = 512
LANES = 128

adapter_scale = 2.0
rate_first = 0.005
rate_second = 0.08
decay_first = 0.05
decay_second = 0.01
neg_large = -1e30
norm_eps = 1e-05
adam_eps = 1e-08

f32 = jnp.float32
bf16 = jnp.bfloat16
sds = jax.ShapeDtypeStruct
VMEM = pltpu.VMEM


def cdot(left, right, left_dim, right_dim, precision=None):
    return lax.dot_general(
        left,
        right,
        (((left_dim,), (right_dim,)), ((), ())),
        precision=precision,
        preferred_element_type=f32,
    )


def low_lanes(shape):
    return lax.broadcasted_iota(jnp.int32, shape, 1) < HEAD_DIM


def head_pair_rows(pair, with_ones):
    low = low_lanes(pair.shape)
    zero = jnp.zeros_like(pair)
    first = jnp.where(low, pair, zero)
    second = jnp.where(low, zero, pair)
    if with_ones:
        one = jnp.ones_like(pair)
        first = jnp.concatenate([first, jnp.where(low, one, zero)], axis=1)
        second = jnp.concatenate([second, jnp.where(low, zero, one)], axis=1)
    return jnp.concatenate([first, second], axis=0)


def row_mean(values):
    return jnp.sum(values, axis=1, keepdims=True) * (1.0 / values.shape[1])


def lane_is_rank(rank):
    shape = (rank, LANES)
    return lax.broadcasted_iota(jnp.int32, shape, 1) % rank == lax.broadcasted_iota(
        jnp.int32, shape, 0
    )


def lane_is_feature(rows, rank):
    shape = (rows, LANES)
    return lax.broadcasted_iota(jnp.int32, shape, 0) % (LANES // rank) == (
        lax.broadcasted_iota(jnp.int32, shape, 1) // rank
    )


def flatten_pair(flat, j, spread, up, scale):
    rank, width = up.shape
    group = LANES // rank
    down_rows = width // group
    part = jnp.where(lane_is_feature(width, rank), spread, 0.0)
    flat[j * down_rows : (j + 1) * down_rows, :] = jnp.sum(
        part.reshape(down_rows, group, LANES), axis=1
    )
    up_rows = width // LANES
    base = 2 * down_rows + j * rank * up_rows
    for cb in range(up_rows):
        flat[pl.ds(base + cb, rank, stride=up_rows), :] = (
            scale * up[:, cb * LANES : (cb + 1) * LANES]
        )


def row_moves(wide, chunk_rows):
    unit = 8 if chunk_rows % 8 == 0 else 1
    for h in range(wide // 2):
        for k in range(0, chunk_rows, unit):
            yield h * chunk_rows + k, 2 * h * chunk_rows + k, unit


def aligned(row, unit):
    return pl.multiple_of(row, unit) if unit > 1 else row


def split_half(flat, out, core, wide):
    chunk_rows = flat.shape[0] // wide
    for at, row, unit in row_moves(wide, chunk_rows):
        out[at : at + unit, :] = flat[pl.ds(aligned(row + core * chunk_rows, unit), unit), :]


def layer_kernel(
    lens,
    x_hbm,
    cot_hbm,
    wq_hbm,
    wk_hbm,
    wv_hbm,
    wo_hbm,
    w1_hbm,
    w2_hbm,
    bq,
    bv,
    bo,
    b1,
    b2,
    gains,
    shifts,
    down_t,
    up,
    mixed_hbm,
    tokg_hbm,
    keep_out,
    send_out,
    x,
    cot,
    wq,
    wk,
    wv,
    wo,
    w1,
    w2,
    acat,
    brep_q,
    brep_v,
    rowv,
    qs,
    ks,
    vs,
    dn,
    probs,
    ctx,
    inv_l,
    dctx,
    act,
    slope,
    mixed,
    tokg,
    midg,
    dq,
    dk,
    dv,
    g_down,
    g_up_q,
    g_up_v,
    flat,
    in_sem,
    w_sem,
    out_sem,
    *,
    wide,
):
    d_model = x.shape[1]
    n_bucket = x.shape[0] // BUCKET
    n_pair = d_model // LANES
    ff = w1.shape[1]
    rank = up.shape[1]
    core = lax.rem(lax.axis_index("wide"), 2)

    def bucket_copy(i, src, dst, sem):
        rows = pl.ds(i * BUCKET, BUCKET)
        return pltpu.make_async_copy(src.at[rows, :], dst.at[rows, :], sem)

    weights = [(wq_hbm, wq), (wk_hbm, wk), (wv_hbm, wv), (wo_hbm, wo), (w1_hbm, w1), (w2_hbm, w2)]
    weight_copies = [pltpu.make_async_copy(s, d, w_sem.at[i]) for i, (s, d) in enumerate(weights)]
    x_copies = [bucket_copy(i, x_hbm, x, in_sem.at[i]) for i in range(n_bucket)]
    cot_copies = [bucket_copy(i, cot_hbm, cot, in_sem.at[n_bucket + i]) for i in range(n_bucket)]
    x_copies[0].start()
    for c in weight_copies[:4]:
        c.start()
    cot_copies[0].start()
    for c in weight_copies[4:]:
        c.start()
    for c in x_copies[1:] + cot_copies[1:]:
        c.start()

    acat[...] = jnp.concatenate(
        [down_t[0], down_t[1], jnp.zeros((LANES - 2 * rank, d_model), f32)], axis=0
    ).astype(bf16)
    up_q = up[0].astype(bf16).astype(f32) * adapter_scale
    up_v = up[1].astype(bf16).astype(f32) * adapter_scale
    brep_q[...] = jnp.concatenate([up_q] * (LANES // rank), axis=0).astype(bf16)
    brep_v[...] = jnp.concatenate([up_v] * (LANES // rank), axis=0).astype(bf16)
    seq = 0
    row0 = 0
    n_valid = 0
    for length in (LEN_A, LEN_B, LEN_C):
        for s in range(BUCKET // length):
            n = lens[seq]
            n_valid = n_valid + n
            rowv[row0 : row0 + length, :] = (
                lax.broadcasted_iota(jnp.int32, (length, LANES), 0) < n
            ).astype(f32)
            seq += 1
            row0 += length
    g_down[...] = jnp.zeros_like(g_down)
    g_up_q[...] = jnp.zeros_like(g_up_q)
    g_up_v[...] = jnp.zeros_like(g_up_v)

    def pair_at(p, row):
        if isinstance(p, int):
            return slice(p * LANES, (p + 1) * LANES), p * BUCKET + row
        return (
            pl.ds(pl.multiple_of(p * LANES, LANES), LANES),
            pl.multiple_of(p * BUCKET + row, LANES),
        )

    def each_pair(per_step, body):
        if per_step == n_pair:
            for p in range(n_pair):
                body(p, p)
            return

        def step_of(i, carry):
            for j in range(per_step):
                body(i * per_step + j, j)
            return carry

        lax.fori_loop(0, n_pair // per_step, step_of, 0)

    def attend(length, first_seq, p, s):
        rows = slice(s * length, (s + 1) * length)
        cols, prow = pair_at(p, s * length)
        key_rows = head_pair_rows(ks[rows, cols], False)
        val_rows = head_pair_rows(vs[rows, cols], True)
        lane = lax.broadcasted_iota(jnp.int32, (1, length), 1)
        bias = jnp.where(lane < lens[first_seq + s], 0.0, neg_large).astype(f32)
        scores = cdot(qs[rows, cols], key_rows, 1, 1)
        parts = []
        for h in range(2):
            sh = scores[:, h * length : (h + 1) * length] + bias
            parts.append(jnp.exp(sh - jnp.max(sh, axis=1, keepdims=True)).astype(bf16))
        e = jnp.concatenate(parts, axis=1)
        probs[pl.ds(prow, length), : 2 * length] = e
        out = cdot(e, val_rows, 1, 0)
        inv = 1.0 / out[:, LANES:]
        inv_l[rows, cols] = inv
        ctx[rows, cols] = (out[:, :LANES] * inv).astype(bf16)

    def attend_back(length, p, s, values_first):
        rows = slice(s * length, (s + 1) * length)
        cols, prow = pair_at(p, s * length)
        key_rows = head_pair_rows(ks[rows, cols], False)
        val_rows = head_pair_rows(vs[rows, cols], True)
        low = low_lanes((length, LANES))
        dcf = dctx[rows, cols].astype(f32) * inv_l[rows, cols]
        dc = dcf.astype(bf16)
        inner = (-dcf * ctx[rows, cols].astype(f32)).astype(bf16)
        e = probs[pl.ds(prow, length), : 2 * length]

        def value_part():
            rv = cdot(e, dc, 0, 0)
            dv[rows, cols] = jnp.where(low, rv[:length], rv[length:]).astype(bf16)

        if values_first:
            value_part()
        g = cdot(jnp.concatenate([dc, inner], axis=1), val_rows, 1, 1)
        ds = (e.astype(f32) * g).astype(bf16)
        dq[rows, cols] = (cdot(ds, key_rows, 1, 0) * (HEAD_DIM**-0.5)).astype(bf16)
        rk = cdot(ds, qs[rows, cols], 0, 0)
        dk[rows, cols] = jnp.where(low, rk[:length], rk[length:]).astype(bf16)
        if not values_first:
            value_part()

    size = 256
    n_chunk = 2
    ahead = (6, 6, 6)
    back = (3, 6, 3)
    step = 256

    def chain(b, first_row):
        chunks = range(n_chunk)
        lrows = [pl.ds(pl.multiple_of(first_row + c * size, size), size) for c in chunks]
        grows = [
            pl.ds(pl.multiple_of(b * BUCKET + first_row + c * size, size), size) for c in chunks
        ]

        def first_norm(c):
            ms = cdot(ctx[lrows[c], :], wo[...], 1, 0) + bo[...][None] + x[grows[c], :].astype(f32)
            xc = ms - row_mean(ms)
            r1 = lax.rsqrt(row_mean(xc * xc) + norm_eps)
            n1 = xc * r1
            return r1, n1, n1 * gains[0:1, :] + shifts[0:1, :]

        def inner_ffn(c, nl):
            for n in range(0, ff, step):
                h = cdot(nl, w1[:, n : n + step], 1, 0) + b1[n : n + step][None]
                cdf = 0.5 + 0.5 * lax.erf(h * (0.5**0.5))
                pdf = jnp.exp(h * h * -0.5) * 0.3989422804014327
                act[lrows[c], n : n + step] = (h * cdf).astype(bf16)
                slope[lrows[c], n : n + step] = (cdf + h * pdf).astype(bf16)

        def second_norm(c, normed):
            fs = cdot(act[lrows[c], :], w2[...], 1, 0) + b2[...][None] + normed
            fc = fs - row_mean(fs)
            r2 = lax.rsqrt(row_mean(fc * fc) + norm_eps)
            n2 = fc * r2
            mixed[lrows[c], :] = (n2 * gains[1:2, :] + shifts[1:2, :]).astype(bf16)
            rv = rowv[grows[c], :]
            e2 = cot[grows[c], :].astype(f32) * jnp.concatenate([rv] * n_pair, axis=1)
            e2 = e2 * gains[1:2, :]
            return r2 * (e2 - row_mean(e2) - n2 * row_mean(e2 * n2))

        def inner_back(c, ol):
            for n in range(0, ff, step):
                da = cdot(ol, w2[n : n + step, :], 1, 1).astype(bf16)
                act[lrows[c], n : n + step] = da * slope[lrows[c], n : n + step]

        def first_back(c, fg, r1, n1):
            e1 = (fg + cdot(act[lrows[c], :], w1[...], 1, 1)) * gains[0:1, :]
            mg = r1 * (e1 - row_mean(e1) - n1 * row_mean(e1 * n1))
            midg[lrows[c], :] = mg
            dctx[lrows[c], :] = cdot(mg.astype(bf16), wo[...], 1, 1).astype(bf16)

        firsts = [first_norm(c) for c in chunks]
        for c in chunks:
            inner_ffn(c, firsts[c][2].astype(bf16))
        grads = [second_norm(c, firsts[c][2]) for c in chunks]
        for c in chunks:
            inner_back(c, grads[c].astype(bf16))
        for c in chunks:
            first_back(c, grads[c], firsts[c][0], firsts[c][1])

    outs = [(mixed, mixed_hbm), (tokg, tokg_hbm)]

    def out_copy(i, b):
        rows = pl.ds(pl.multiple_of(b * BUCKET, BUCKET), BUCKET)
        src, dst = outs[i]
        return pltpu.make_async_copy(src, dst.at[rows, :], out_sem.at[i])

    def out_free(which, b):
        @pl.when(b > 0)
        def _():
            for i in which:
                out_copy(i, b - 1).wait()

    def bucket(b, carry):
        rows = pl.ds(pl.multiple_of(b * BUCKET, BUCKET), BUCKET)

        def wait_bucket(src, dst, base):
            pltpu.make_async_copy(src.at[rows, :], dst.at[rows, :], in_sem.at[base + b]).wait()

        wait_bucket(x_hbm, x, 0)

        @pl.when(b == 0)
        def _():
            for i, (w, low, high) in enumerate(((wq, down_t[0], up_q), (wk, None, None), (wv, down_t[1], up_v))):
                weight_copies[i].wait()
                if low is not None:
                    w[...] = (
                        w[...].astype(f32) + cdot(low.astype(bf16), high.astype(bf16), 0, 0)
                    ).astype(bf16)

        xb = x[rows, :]
        dnb = cdot(xb, acat[...], 1, 1).astype(bf16)
        dn[...] = dnb
        qs[...] = (cdot(xb, wq[...], 1, 0) + bq[...][None]).astype(bf16) * jnp.asarray(
            HEAD_DIM**-0.5, bf16
        )
        ks[...] = cdot(xb, wk[...], 1, 0).astype(bf16)
        vs[...] = (cdot(xb, wv[...], 1, 0) + bv[...][None]).astype(bf16)

        first = 0
        for i, length in enumerate((LEN_A, LEN_B, LEN_C)):
            count = BUCKET // length

            @pl.when(b == i)
            def _(i=i, length=length, first=first, count=count):
                def both(p, place):
                    for s in range(count):
                        attend(length, first, p, s)

                each_pair(ahead[i], both)

            first += count

        wait_bucket(cot_hbm, cot, n_bucket)

        @pl.when(b == 0)
        def _():
            for c in weight_copies[3:]:
                c.wait()

        out_free((0,), b)

        def chunk(c, carry):
            chain(b, c * (size * n_chunk))
            return carry

        lax.fori_loop(0, BUCKET // (size * n_chunk), chunk, 0)
        out_copy(0, b).start()

        for i, length in enumerate((LEN_A, LEN_B, LEN_C)):
            count = BUCKET // length

            @pl.when(b == i)
            def _(i=i, length=length, count=count):
                def both(p, place):
                    for s in range(count):
                        attend_back(length, p, s, (place * count + s) % 2 == 1)

                each_pair(back[i], both)

        out_free((1,), b)
        dqb = dq[...]
        dvb = dv[...]
        dgb = jnp.concatenate(
            [cdot(dqb, brep_q[...], 1, 1).astype(bf16), cdot(dvb, brep_v[...], 1, 1).astype(bf16)],
            axis=1,
        )
        g_down[...] += cdot(x[rows, :], dgb, 0, 0)
        dnb2 = dn[...]
        g_up_q[...] += cdot(dnb2, dqb, 0, 0)
        g_up_v[...] += cdot(dnb2, dvb, 0, 0)
        tokg[...] = (
            cdot(dqb, wq[...], 1, 1)
            + cdot(dk[...], wk[...], 1, 1)
            + cdot(dvb, wv[...], 1, 1)
            + midg[...]
        ).astype(bf16)
        out_copy(1, b).start()
        return carry

    lax.fori_loop(0, n_bucket, bucket, 0)

    for j, src in enumerate((g_up_q, g_up_v)):
        flatten_pair(
            flat,
            j,
            g_down[:, j * LANES : (j + 1) * LANES],
            src[j * rank : (j + 1) * rank, :],
            adapter_scale,
        )
    n_rows = flat.shape[0]
    split_half(flat, keep_out, core, wide)
    split_half(flat, send_out, 1 - core, wide)
    total = jnp.full((8, LANES), n_valid, jnp.int32).astype(f32)
    keep_out[n_rows // 2 :, :] = total
    send_out[n_rows // 2 :, :] = total
    for i in range(len(outs)):
        out_copy(i, n_bucket - 1).wait()


def layer(lens, x, cot, ws, vecs, gains, shifts, down_t, up, wide):
    t, d = x.shape
    ff = ws[4].shape[1]
    rank = up.shape[1]
    n_rows = 2 * down_t.size // LANES
    n_bucket = t // BUCKET
    any_spec = pl.BlockSpec(memory_space=pl.ANY)
    vm = pl.BlockSpec(memory_space=VMEM)
    ops = [lens, x, cot, *ws, *vecs, gains, shifts, down_t, up]
    in_specs = (
        [pl.BlockSpec(memory_space=pltpu.SMEM)] + [any_spec] * 8 + [vm] * (len(vecs) + 4)
    )
    out_shape = [
        sds((t, d), bf16),
        sds((t, d), bf16),
        sds((n_rows // 2 + 8, LANES), f32),
        sds((n_rows // 2 + 8, LANES), f32),
    ]
    dma = pltpu.SemaphoreType.DMA
    scratch = [
        VMEM((t, d), bf16),
        VMEM((t, d), bf16),
        VMEM((d, d), bf16),
        VMEM((d, d), bf16),
        VMEM((d, d), bf16),
        VMEM((d, d), bf16),
        VMEM((d, ff), bf16),
        VMEM((ff, d), bf16),
        VMEM((LANES, d), bf16),
        VMEM((LANES, d), bf16),
        VMEM((LANES, d), bf16),
        VMEM((t, LANES), f32),
        VMEM((BUCKET, d), bf16),
        VMEM((BUCKET, d), bf16),
        VMEM((BUCKET, d), bf16),
        VMEM((BUCKET, LANES), bf16),
        VMEM((d // LANES * BUCKET, 2 * LEN_C), bf16),
        VMEM((BUCKET, d), bf16),
        VMEM((BUCKET, d), f32),
        VMEM((BUCKET, d), bf16),
        VMEM((BUCKET, ff), bf16),
        VMEM((BUCKET, ff), bf16),
        VMEM((BUCKET, d), bf16),
        VMEM((BUCKET, d), bf16),
        VMEM((BUCKET, d), f32),
        VMEM((BUCKET, d), bf16),
        VMEM((BUCKET, d), bf16),
        VMEM((BUCKET, d), bf16),
        VMEM((d, 2 * LANES), f32),
        VMEM((LANES, d), f32),
        VMEM((LANES, d), f32),
        VMEM((n_rows, LANES), f32),
        dma((2 * n_bucket,)),
        dma((6,)),
        dma((2,)),
    ]
    body = lambda *refs: layer_kernel(*refs, wide=wide)
    return pl.pallas_call(
        body,
        out_shape=out_shape,
        in_specs=in_specs,
        out_specs=[any_spec] * 2 + [vm] * 2,
        scratch_shapes=scratch,
        compiler_params=pltpu.CompilerParams(vmem_limit_bytes=63 << 20),
        name="layer",
    )(*ops)


def update_kernel(
    beta_one, beta_two, step, own, other, down_t, up, new_down_t, new_up, first_out, second_out, *scratch, n, held, wide, low
):
    grads, first, second, moves = scratch
    rank, width = up.shape[1:]
    n_rows = grads.shape[0]
    rows = n_rows // 2
    chunk_rows = n_rows // wide
    place = lax.axis_index("wide")
    core = lax.rem(place, 2)
    digit = (place >> low) % n
    unit = 8 if chunk_rows % 8 == 0 else 1

    def put(dst, chunk, src, at):
        for k in range(0, chunk_rows, unit):
            row = aligned(chunk * chunk_rows + k, unit)
            dst[pl.ds(row, unit), :] = src[at + k : at + k + unit, :]

    block = held * chunk_rows
    for src, parity in ((own, core), (other, 1 - core)):
        for h in range(wide // 2):
            put(grads, 2 * h + parity, src, h * chunk_rows)
        for j in range(n):
            for i in range(held):
                chunk = 2 * ((digit ^ j) * held + i) + parity
                at = rows + 8 + 2 * j * block + i * chunk_rows
                put(first, chunk, src, at)
                put(second, chunk, src, at + block)
    gradient = grads[...] / own[rows : rows + 1, :]
    b1 = jnp.full((8, LANES), beta_one[0], f32)
    b2 = jnp.full((8, LANES), beta_two[0], f32)
    count = step[0]
    power1 = jnp.ones((8, LANES), f32)
    power2 = power1
    square1, square2 = b1, b2
    for bit in range(16):
        on = ((count >> bit) & 1) == 1
        power1 = jnp.where(on, power1 * square1, power1)
        power2 = jnp.where(on, power2 * square2, power2)
        square1 = square1 * square1
        square2 = square2 * square2
    b1, b2 = b1[:1], b2[:1]
    m = b1 * first[...] + (1.0 - b1) * gradient
    v = b2 * second[...] + (1.0 - b2) * gradient * gradient
    first[...] = m
    second[...] = v
    moves[...] = (m / (1.0 - power1[:1])) / (jnp.sqrt(v / (1.0 - power2[:1])) + adam_eps)
    for k in range(0, chunk_rows, unit):
        at = aligned(place * chunk_rows + k, unit)
        first_out[k : k + unit, :] = first[pl.ds(at, unit), :]
        second_out[k : k + unit, :] = second[pl.ds(at, unit), :]
    group = LANES // rank
    down_rows = width // group
    up_rows = width // LANES
    for j in range(2):
        spread = jnp.broadcast_to(
            moves[j * down_rows : (j + 1) * down_rows, :][:, None, :], (down_rows, group, LANES)
        ).reshape(width, LANES)
        part = jnp.where(lane_is_feature(width, rank), spread, 0.0)
        move = cdot(lane_is_rank(rank).astype(f32), part, 1, 1, lax.Precision.HIGHEST)
        new_down_t[j] = down_t[j] * (1.0 - rate_first * decay_first) - rate_first * move
        base = 2 * down_rows + j * rank * up_rows
        for cb in range(up_rows):
            cols = slice(cb * LANES, (cb + 1) * LANES)
            new_up[j, :, cols] = up[j, :, cols] * (1.0 - rate_second * decay_second) - (
                rate_second * moves[pl.ds(base + cb, rank, stride=up_rows), :]
            )


def update(beta_one, beta_two, step, own, other, down_t, up, n, held, wide, low):
    n_rows = 2 * down_t.size // LANES
    chunk_rows = n_rows // wide
    smem = pl.BlockSpec(memory_space=pltpu.SMEM)
    vm = pl.BlockSpec(memory_space=VMEM)
    return pl.pallas_call(
        lambda *refs: update_kernel(*refs, n=n, held=held, wide=wide, low=low),
        out_shape=[
            sds(down_t.shape, f32),
            sds(up.shape, f32),
            sds((chunk_rows, LANES), f32),
            sds((chunk_rows, LANES), f32),
        ],
        in_specs=[smem] * 3 + [vm] * 4,
        out_specs=[vm] * 4,
        scratch_shapes=[VMEM((n_rows, LANES), f32)] * 4,
        compiler_params=pltpu.CompilerParams(vmem_limit_bytes=16 << 20),
        name="update",
    )(beta_one, beta_two, step, own, other, down_t, up)


def digit_groups(size, first):
    bits = size.bit_length() - 1
    groups = []
    at = first
    while at < bits:
        n = min(2, bits - at)
        groups.append((at, n))
        at += n
    return groups


def swap_perm(size, mask):
    return [(i, i ^ mask) for i in range(size)]


def exchange(values, axis, size, group):
    low, n = group
    return [values] + [
        lax.ppermute(values, axis, swap_perm(size, j << low)) for j in range(1, 1 << n)
    ]


def tree_sum(parts):
    while len(parts) > 1:
        parts = [parts[i] + parts[i + 1] for i in range(0, len(parts), 2)]
    return parts[0]


def in_order(parts, digit):
    parts = list(parts)
    n = len(parts).bit_length() - 1
    for bit in range(n):
        flip = (digit >> bit) & 1
        parts = [jnp.where(flip == 1, parts[i ^ (1 << bit)], parts[i]) for i in range(len(parts))]
    return parts


def per_device(
    tokens,
    cotangent,
    valid_token_length,
    query_weight_matrix,
    key_weight_matrix,
    value_weight_matrix,
    attention_output_weight,
    inner_ffn_weight,
    outer_ffn_weight,
    query_bias_vector,
    value_bias_vector,
    attention_output_bias,
    hidden_ffn_bias,
    ffn_output_bias,
    layer_norm_gains,
    layer_norm_biases,
    adapter_down_factors,
    adapter_up_factors,
    first_moment_estimate,
    second_moment_estimate,
    first_decay_factor,
    second_decay_factor,
    optimizer_step_number,
):
    dp = lax.axis_size("dp")
    wide = lax.axis_size("wide")
    place = lax.axis_index("wide")
    n_rows = 2 * adapter_down_factors.size // LANES
    chunk_rows = n_rows // wide

    down_t = jnp.swapaxes(adapter_down_factors, 1, 2)
    mixed, token_grad, keep, send = layer(
        valid_token_length,
        tokens,
        cotangent,
        (
            query_weight_matrix,
            key_weight_matrix,
            value_weight_matrix,
            attention_output_weight,
            inner_ffn_weight,
            outer_ffn_weight,
        ),
        (
            query_bias_vector,
            value_bias_vector,
            attention_output_bias,
            hidden_ffn_bias,
            ffn_output_bias,
        ),
        layer_norm_gains,
        layer_norm_biases,
        down_t,
        adapter_up_factors,
        wide,
    )

    grad = keep + lax.ppermute(send, "wide", swap_perm(wide, 1))
    for group in digit_groups(dp, 0):
        grad = tree_sum(exchange(grad, "dp", dp, group))

    first = first_moment_estimate.reshape(chunk_rows, LANES)
    second = second_moment_estimate.reshape(chunk_rows, LANES)
    held = 1
    rows = n_rows // 2 + 8
    groups = digit_groups(wide, 1)
    for i, (low, n) in enumerate(groups):
        pieces = exchange(jnp.concatenate([grad, first, second], axis=0), "wide", wide, (low, n))
        grad = tree_sum([p[:rows] for p in pieces])
        if i + 1 < len(groups):
            block = held * chunk_rows
            pieces = in_order(pieces, place >> low)
            first = jnp.concatenate([p[rows : rows + block] for p in pieces], axis=0)
            second = jnp.concatenate([p[rows + block :] for p in pieces], axis=0)
            held *= len(pieces)
    own = jnp.concatenate([grad] + [p[rows:] for p in pieces], axis=0)
    other = lax.ppermute(own, "wide", swap_perm(wide, 1))
    low, n = groups[-1]
    updated_down_t, updated_up, updated_first, updated_second = update(
        first_decay_factor,
        second_decay_factor,
        optimizer_step_number,
        own,
        other,
        down_t,
        adapter_up_factors,
        1 << n,
        held,
        wide,
        low,
    )
    return (
        mixed,
        token_grad,
        jnp.swapaxes(updated_down_t, 1, 2),
        updated_up,
        updated_first.reshape(-1),
        updated_second.reshape(-1),
    )


def solution(mesh):
    rows = P(("dp", "wide"), None)
    placed = (rows, rows, P(("dp", "wide"))) + (P(),) * 15 + (P("wide"), P("wide")) + (P(),) * 3
    return jax.shard_map(
        per_device,
        mesh=mesh,
        in_specs=placed,
        out_specs=(rows, rows, P(), P(), P("wide"), P("wide")),
        check_vma=False,
    )
```

time: 137 us -> 113 us (0.82)
  Pallas kernels: 119 us -> 87.6 us
  waiting for transfers between devices: 2.35 us -> 11.2 us
    pallas_call x4 -> x1, Pallas kernels: 19.3 us -> 1.45 us  [update(): pl.pallas_call(lambda *refs: update_kernel(*refs, n=n, held=held, wide=wi...]
    pallas_call x1, Pallas kernels: 99.6 us -> 86.2 us  [layer(): pl.pallas_call(body, out_shape=out_shape, in_specs=in_specs, out_specs=[a...]
    ppermute x6, waiting for transfers between devices: 0.95 us -> 9.82 us  [exchange(): lax.ppermute(values, axis, swap_perm(size, j << low))]
  transfers between devices with their start and end apart: 8 -> 8, of which waited for: 3 -> 6; matrix products, arithmetic and copies ran while one was open for 0% -> 0% of each run, Pallas kernels for 11% -> 0%
where the time goes in v2:
time: 113 us
  Pallas kernels  87.6 us (78%)
  waiting for transfers between devices  11.2 us (10%)
  starting transfers between devices  10.3 us (9%)
  between operations  2.72 us (2%)
    pallas_call x1, Pallas kernels, layer(): pl.pallas_call(body, out_shape=out_shape, in_specs=in_specs, out_specs=[a...  86.2 us
    ppermute x6, waiting for transfers between devices, exchange(): lax.ppermute(values, axis, swap_perm(size, j << low))  9.82 us
    ppermute x6, starting transfers between devices, exchange(): lax.ppermute(values, axis, swap_perm(size, j << low))  7.3 us
    ppermute x1, starting transfers between devices, per_device(): other = lax.ppermute(own, 'wide', swap_perm(wide, 1))  2.92 us
  transfers between devices with their start and end apart: 8, of which 6 were waited for; matrix products, arithmetic and copies ran while one was open for 0% of the time, Pallas kernels for 0%

profile of v2, /device:TPU:1, one launch (start us, length us, event | category | flops | bytes accessed | tf_op | source)
XLA Modules:
  0.0 112.8 jit_solution(8956625380885475594)
XLA Ops:
  0.6 0.0 copy-start.2
  0.6 0.0 copy-start.3
  0.7 0.0 copy-start
  0.7 0.0 copy-start.1
  0.7 86.2 %layer.1 = (bf16[1536,768]{1,0:T(8,128)(2,1)}, bf16[1536,768]{1,0:T(8,128)(2,1)}, f32[104,128]{1,0:T(8,128)}, f32[104,128]{1,0:T(8,128)}) custom-call(s32[7]{0:T(128)} %refs_0_.2, bf16[1536,768]{1,0:T(8,128)(2,1)} %refs_1_.2, bf16[1536,768]{1,0:T(8,128)(2,1)} %refs_2_.2, bf16[768,768]{1,0:T(8,128)(2,1)} %refs_3_.1, bf16[768,768]{1,0:T(8,128)(2,1)} %refs_4_.1, ...), custom_call_target="tpu_custom_call" | custom-call | tf_op jit(solution)/shard_map/layer/pallas_call | solution.py:517
  86.9 0.1 collective-permute-start
  87.0 1.4 %collective-permute-done = f32[104,128]{1,0:T(8,128)S(1)} collective-permute-done((f32[104,128]{1,0:T(8,128)}, f32[104,128]{1,0:T(8,128)S(1)}, u32[]{:S(2)}, u32[]{:S(2)}) %collective-permute-start) | collective-permute-done | bytes 53280 | tf_op jit(solution)/shard_map/ppermute | solution.py:713
  88.4 0.8 add.21
  89.2 2.4 %collective-permute-start.1 = (f32[104,128]{1,0:T(8,128)S(1)}, f32[104,128]{1,0:T(8,128)S(1)}, u32[]{:S(2)}, u32[]{:S(2)}) collective-permute-start(f32[104,128]{1,0:T(8,128)S(1)} %add.21), channel_id=1, source_target_pairs={{0,8},{8,0},{16,24},{24,16},{1,9},{9,1},{17,25},{25,17},{2,10},{10... | collective-permute-start | bytes 159752 | tf_op jit(solution)/shard_map/ppermute | solution.py:636
  91.6 1.2 %collective-permute-start.2 = (f32[104,128]{1,0:T(8,128)S(1)}, f32[104,128]{1,0:T(8,128)S(1)}, u32[]{:S(2)}, u32[]{:S(2)}) collective-permute-start(f32[104,128]{1,0:T(8,128)S(1)} %add.21), channel_id=1, source_target_pairs={{0,16},{8,24},{16,0},{24,8},{1,17},{9,25},{17,1},{25,9},{2,18},{10... | collective-permute-start | bytes 159752 | tf_op jit(solution)/shard_map/ppermute | solution.py:636
  92.8 0.0 collective-permute-start.3
  92.8 0.7 collective-permute-done.1
  93.5 1.1 collective-permute-done.2
  94.6 2.1 %collective-permute-done.3 = f32[104,128]{1,0:T(8,128)S(1)} collective-permute-done((f32[104,128]{1,0:T(8,128)S(1)}, f32[104,128]{1,0:T(8,128)S(1)}, u32[]{:S(2)}, u32[]{:S(2)}) %collective-permute-start.3) | collective-permute-done | bytes 53280 | tf_op jit(solution)/shard_map/ppermute | solution.py:636
  96.7 0.0 copy-done.3
  96.8 1.4 %collective-permute-start.4 = (f32[152,128]{1,0:T(8,128)S(1)}, f32[152,128]{1,0:T(8,128)S(1)}, u32[]{:S(2)}, u32[]{:S(2)}) collective-permute-start(f32[152,128]{1,0:T(8,128)S(1)} %pad_maximum_fusion), channel_id=1, source_target_pairs={{0,2},{1,3},{2,0},{3,1},{4,6},{5,7},{6,4},{7,5},{8,10},{9,11},{10,... | collective-permute-start | bytes 233480 | tf_op jit(solution)/shard_map/ppermute | solution.py:636
  98.1 2.3 %collective-permute-start.5 = (f32[152,128]{1,0:T(8,128)S(1)}, f32[152,128]{1,0:T(8,128)S(1)}, u32[]{:S(2)}, u32[]{:S(2)}) collective-permute-start(f32[152,128]{1,0:T(8,128)S(1)} %pad_maximum_fusion), channel_id=1, source_target_pairs={{0,4},{1,5},{2,6},{3,7},{4,0},{5,1},{6,2},{7,3},{8,12},{9,13},{10,... | collective-permute-start | bytes 233480 | tf_op jit(solution)/shard_map/ppermute | solution.py:636
  100.4 0.0 collective-permute-start.6
  100.4 0.0 collective-permute-done.4
  100.4 2.7 %collective-permute-done.5 = f32[152,128]{1,0:T(8,128)S(1)} collective-permute-done((f32[152,128]{1,0:T(8,128)S(1)}, f32[152,128]{1,0:T(8,128)S(1)}, u32[]{:S(2)}, u32[]{:S(2)}) %collective-permute-start.5) | collective-permute-done | bytes 77856 | tf_op jit(solution)/shard_map/ppermute | solution.py:636
  103.1 3.3 %collective-permute-done.6 = f32[152,128]{1,0:T(8,128)S(1)} collective-permute-done((f32[152,128]{1,0:T(8,128)S(1)}, f32[152,128]{1,0:T(8,128)S(1)}, u32[]{:S(2)}, u32[]{:S(2)}) %collective-permute-start.6) | collective-permute-done | bytes 77856 | tf_op jit(solution)/shard_map/ppermute | solution.py:636
  106.5 2.9 %collective-permute-start.7 = (f32[296,128]{1,0:T(8,128)S(1)}, f32[296,128]{1,0:T(8,128)S(1)}, u32[]{:S(2)}, u32[]{:S(2)}) collective-permute-start(f32[296,128]{1,0:T(8,128)S(1)} %slice_dynamic-update-slice_fusion.refs_3_), channel_id=1, source_target_pairs={{0,1},{1,0},{2,3},{3,2},{4,5},{5,4},{6,7},{7,6},{8,9},{9,8},{10,11... | collective-permute-start | bytes 454664 | tf_op jit(solution)/shard_map/ppermute | solution.py:732
  111.3 0.0 collective-permute-done.7.refs_4_
  111.4 1.4 %update.1 = (f32[2,8,768]{2,1,0:T(8,128)}, f32[2,8,768]{2,1,0:T(8,128)}, f32[24,128]{1,0:T(8,128)}, f32[24,128]{1,0:T(8,128)}) custom-call(f32[1]{0:T(128)S(6)} %copy.34.refs_0_, f32[1]{0:T(128)S(6)} %copy.35.refs_1_, s32[1]{0:T(128)S(6)} %copy.36.refs_2_, f32[296,128]{1,0:T(8,128)S(1)} %slice_dynamic-update-slice_fusion.refs_3_, ...), custom_call_target="tpu_custom_call" | custom-call | tf_op jit(solution)/shard_map/update/pallas_call | solution.py:602
  (11 shorter events, 0.1 us)
Async XLA Ops:
  0.6 96.1 %copy-start.2 = (f32[3072]{0:T(1024)S(1)}, f32[3072]{0:T(1024)}, u32[]{:S(2)}) copy-start(f32[3072]{0:T(1024)} %param.41) | copy-start | bytes 36868
  0.6 96.1 %copy-start.3 = (f32[3072]{0:T(1024)S(1)}, f32[3072]{0:T(1024)}, u32[]{:S(2)}) copy-start(f32[3072]{0:T(1024)} %param.42) | copy-start | bytes 36868
  0.7 110.7 %copy-start = (f32[2,768,8]{1,2,0:T(8,128)S(1)}, f32[2,768,8]{1,2,0:T(8,128)}, u32[]{:S(2)}) copy-start(f32[2,768,8]{1,2,0:T(8,128)} %param.39) | copy-start | bytes 147460
  0.7 110.7 %copy-start.1 = (f32[2,8,768]{2,1,0:T(8,128)S(1)}, f32[2,8,768]{2,1,0:T(8,128)}, u32[]{:S(2)}) copy-start(f32[2,8,768]{2,1,0:T(8,128)} %refs_6_.3) | copy-start | bytes 147460
  86.9 1.5 %collective-permute-start = (f32[104,128]{1,0:T(8,128)}, f32[104,128]{1,0:T(8,128)S(1)}, u32[]{:S(2)}, u32[]{:S(2)}) collective-permute-start(f32[104,128]{1,0:T(8,128)} %get-tuple-element.17), channel_id=1, source_target_pairs={{0,1},{1,0},{2,3},{3,2},{4,5},{5,4},{6,7},{7,6},{8,9},{9,8},{10,11... | collective-permute-start | bytes 159752 | tf_op jit(solution)/shard_map/ppermute | solution.py:713
  89.2 4.3 %collective-permute-start.1 = (f32[104,128]{1,0:T(8,128)S(1)}, f32[104,128]{1,0:T(8,128)S(1)}, u32[]{:S(2)}, u32[]{:S(2)}) collective-permute-start(f32[104,128]{1,0:T(8,128)S(1)} %add.21), channel_id=1, source_target_pairs={{0,8},{8,0},{16,24},{24,16},{1,9},{9,1},{17,25},{25,17},{2,10},{10... | collective-permute-start | bytes 159752 | tf_op jit(solution)/shard_map/ppermute | solution.py:636
  91.6 3.0 %collective-permute-start.2 = (f32[104,128]{1,0:T(8,128)S(1)}, f32[104,128]{1,0:T(8,128)S(1)}, u32[]{:S(2)}, u32[]{:S(2)}) collective-permute-start(f32[104,128]{1,0:T(8,128)S(1)} %add.21), channel_id=1, source_target_pairs={{0,16},{8,24},{16,0},{24,8},{1,17},{9,25},{17,1},{25,9},{2,18},{10... | collective-permute-start | bytes 159752 | tf_op jit(solution)/shard_map/ppermute | solution.py:636
  92.8 3.9 %collective-permute-start.3 = (f32[104,128]{1,0:T(8,128)S(1)}, f32[104,128]{1,0:T(8,128)S(1)}, u32[]{:S(2)}, u32[]{:S(2)}) collective-permute-start(f32[104,128]{1,0:T(8,128)S(1)} %add.21), channel_id=1, source_target_pairs={{0,24},{8,16},{16,8},{24,0},{1,25},{9,17},{17,9},{25,1},{2,26},{10... | collective-permute-start | bytes 159752 | tf_op jit(solution)/shard_map/ppermute | solution.py:636
  96.8 3.7 %collective-permute-start.4 = (f32[152,128]{1,0:T(8,128)S(1)}, f32[152,128]{1,0:T(8,128)S(1)}, u32[]{:S(2)}, u32[]{:S(2)}) collective-permute-start(f32[152,128]{1,0:T(8,128)S(1)} %pad_maximum_fusion), channel_id=1, source_target_pairs={{0,2},{1,3},{2,0},{3,1},{4,6},{5,7},{6,4},{7,5},{8,10},{9,11},{10,... | collective-permute-start | bytes 233480 | tf_op jit(solution)/shard_map/ppermute | solution.py:636
  98.1 5.0 %collective-permute-start.5 = (f32[152,128]{1,0:T(8,128)S(1)}, f32[152,128]{1,0:T(8,128)S(1)}, u32[]{:S(2)}, u32[]{:S(2)}) collective-permute-start(f32[152,128]{1,0:T(8,128)S(1)} %pad_maximum_fusion), channel_id=1, source_target_pairs={{0,4},{1,5},{2,6},{3,7},{4,0},{5,1},{6,2},{7,3},{8,12},{9,13},{10,... | collective-permute-start | bytes 233480 | tf_op jit(solution)/shard_map/ppermute | solution.py:636
  100.4 6.0 %collective-permute-start.6 = (f32[152,128]{1,0:T(8,128)S(1)}, f32[152,128]{1,0:T(8,128)S(1)}, u32[]{:S(2)}, u32[]{:S(2)}) collective-permute-start(f32[152,128]{1,0:T(8,128)S(1)} %pad_maximum_fusion), channel_id=1, source_target_pairs={{0,6},{1,7},{2,4},{3,5},{4,2},{5,3},{6,0},{7,1},{8,14},{9,15},{10,... | collective-permute-start | bytes 233480 | tf_op jit(solution)/shard_map/ppermute | solution.py:636
  106.5 4.9 %collective-permute-start.7 = (f32[296,128]{1,0:T(8,128)S(1)}, f32[296,128]{1,0:T(8,128)S(1)}, u32[]{:S(2)}, u32[]{:S(2)}) collective-permute-start(f32[296,128]{1,0:T(8,128)S(1)} %slice_dynamic-update-slice_fusion.refs_3_), channel_id=1, source_target_pairs={{0,1},{1,0},{2,3},{3,2},{4,5},{5,4},{6,7},{7,6},{8,9},{9,8},{10,11... | collective-permute-start | bytes 454664 | tf_op jit(solution)/shard_map/ppermute | solution.py:732

commit v3 on v2

--- a/solution.py
+++ b/solution.py
@@ -125,7 +125,12 @@
     down_t,
     up,
     mixed_hbm,
-    tokg_hbm,
+    midg_hbm,
+    dq_hbm,
+    dk_hbm,
+    dv_hbm,
+    wq_out,
+    wv_out,
     keep_out,
     send_out,
     x,
@@ -151,7 +156,6 @@
     act,
     slope,
     mixed,
-    tokg,
     midg,
     dq,
     dk,
@@ -181,14 +185,15 @@
     weight_copies = [pltpu.make_async_copy(s, d, w_sem.at[i]) for i, (s, d) in enumerate(weights)]
     x_copies = [bucket_copy(i, x_hbm, x, in_sem.at[i]) for i in range(n_bucket)]
     cot_copies = [bucket_copy(i, cot_hbm, cot, in_sem.at[n_bucket + i]) for i in range(n_bucket)]
-    x_copies[0].start()
+    x_copies[-1].start()
     for c in weight_copies[:4]:
         c.start()
-    cot_copies[0].start()
+    cot_copies[-1].start()
     for c in weight_copies[4:]:
         c.start()
-    for c in x_copies[1:] + cot_copies[1:]:
-        c.start()
+    for i in reversed(range(n_bucket - 1)):
+        x_copies[i].start()
+        cot_copies[i].start()
 
     acat[...] = jnp.concatenate(
         [down_t[0], down_t[1], jnp.zeros((LANES - 2 * rank, d_model), f32)], axis=0
@@ -278,18 +283,14 @@
         if not values_first:
             value_part()
 
-    size = 256
-    n_chunk = 2
+    size = BUCKET // 2
     ahead = (6, 6, 6)
-    back = (3, 6, 3)
+    back = (6, 3, 3)
     step = 256
 
-    def chain(b, first_row):
-        chunks = range(n_chunk)
-        lrows = [pl.ds(pl.multiple_of(first_row + c * size, size), size) for c in chunks]
-        grows = [
-            pl.ds(pl.multiple_of(b * BUCKET + first_row + c * size, size), size) for c in chunks
-        ]
+    def chain(b):
+        lrows = [slice(c * size, (c + 1) * size) for c in range(2)]
+        grows = [pl.ds(pl.multiple_of(b * BUCKET + c * size, size), size) for c in range(2)]
 
         def first_norm(c):
             ms = cdot(ctx[lrows[c], :], wo[...], 1, 0) + bo[...][None] + x[grows[c], :].astype(f32)
@@ -325,19 +326,26 @@
         def first_back(c, fg, r1, n1):
             e1 = (fg + cdot(act[lrows[c], :], w1[...], 1, 1)) * gains[0:1, :]
             mg = r1 * (e1 - row_mean(e1) - n1 * row_mean(e1 * n1))
-            midg[lrows[c], :] = mg
-            dctx[lrows[c], :] = cdot(mg.astype(bf16), wo[...], 1, 1).astype(bf16)
-
-        firsts = [first_norm(c) for c in chunks]
-        for c in chunks:
-            inner_ffn(c, firsts[c][2].astype(bf16))
-        grads = [second_norm(c, firsts[c][2]) for c in chunks]
-        for c in chunks:
-            inner_back(c, grads[c].astype(bf16))
-        for c in chunks:
-            first_back(c, grads[c], firsts[c][0], firsts[c][1])
-
-    outs = [(mixed, mixed_hbm), (tokg, tokg_hbm)]
+            low = mg.astype(bf16)
+            midg[lrows[c], :] = low
+            dctx[lrows[c], :] = cdot(low, wo[...], 1, 1).astype(bf16)
+
+        r1_a, n1_a, normed_a = first_norm(0)
+        r1_b, n1_b, normed_b = first_norm(1)
+        inner_ffn(0, normed_a.astype(bf16))
+        grad_a = second_norm(0, normed_a)
+        inner_ffn(1, normed_b.astype(bf16))
+        inner_back(0, grad_a.astype(bf16))
+        grad_b = second_norm(1, normed_b)
+        first_back(0, grad_a, r1_a, n1_a)
+        inner_back(1, grad_b.astype(bf16))
+        first_back(1, grad_b, r1_b, n1_b)
+
+    outs = [(mixed, mixed_hbm), (midg, midg_hbm), (dq, dq_hbm), (dk, dk_hbm), (dv, dv_hbm)]
+    folded = [(wq, wq_out), (wv, wv_out)]
+    folded_copies = [
+        pltpu.make_async_copy(s, d, out_sem.at[len(outs) + i]) for i, (s, d) in enumerate(folded)
+    ]
 
     def out_copy(i, b):
         rows = pl.ds(pl.multiple_of(b * BUCKET, BUCKET), BUCKET)
@@ -345,12 +353,13 @@
         return pltpu.make_async_copy(src, dst.at[rows, :], out_sem.at[i])
 
     def out_free(which, b):
-        @pl.when(b > 0)
+        @pl.when(b < n_bucket - 1)
         def _():
             for i in which:
-                out_copy(i, b - 1).wait()
-
-    def bucket(b, carry):
+                out_copy(i, b + 1).wait()
+
+    def bucket(step_b, carry):
+        b = n_bucket - 1 - step_b
         rows = pl.ds(pl.multiple_of(b * BUCKET, BUCKET), BUCKET)
 
         def wait_bucket(src, dst, base):
@@ -358,7 +367,7 @@
 
         wait_bucket(x_hbm, x, 0)
 
-        @pl.when(b == 0)
+        @pl.when(step_b == 0)
         def _():
             for i, (w, low, high) in enumerate(((wq, down_t[0], up_q), (wk, None, None), (wv, down_t[1], up_v))):
                 weight_copies[i].wait()
@@ -366,6 +375,8 @@
                     w[...] = (
                         w[...].astype(f32) + cdot(low.astype(bf16), high.astype(bf16), 0, 0)
                     ).astype(bf16)
+            for c in folded_copies:
+                c.start()
 
         xb = x[rows, :]
         dnb = cdot(xb, acat[...], 1, 1).astype(bf16)
@@ -392,19 +403,17 @@
 
         wait_bucket(cot_hbm, cot, n_bucket)
 
-        @pl.when(b == 0)
+        @pl.when(step_b == 0)
         def _():
             for c in weight_copies[3:]:
                 c.wait()
 
-        out_free((0,), b)
-
-        def chunk(c, carry):
-            chain(b, c * (size * n_chunk))
-            return carry
-
-        lax.fori_loop(0, BUCKET // (size * n_chunk), chunk, 0)
-        out_copy(0, b).start()
+        out_free((0, 1), b)
+
+        chain(b)
+        for i in (0, 1):
+            out_copy(i, b).start()
+        out_free((2, 3, 4), b)
 
         for i, length in enumerate((LEN_A, LEN_B, LEN_C)):
             count = BUCKET // length
@@ -417,7 +426,8 @@
 
                 each_pair(back[i], both)
 
-        out_free((1,), b)
+        for i in (2, 3, 4):
+            out_copy(i, b).start()
         dqb = dq[...]
         dvb = dv[...]
         dgb = jnp.concatenate(
@@ -428,13 +438,6 @@
         dnb2 = dn[...]
         g_up_q[...] += cdot(dnb2, dqb, 0, 0)
         g_up_v[...] += cdot(dnb2, dvb, 0, 0)
-        tokg[...] = (
-            cdot(dqb, wq[...], 1, 1)
-            + cdot(dk[...], wk[...], 1, 1)
-            + cdot(dvb, wv[...], 1, 1)
-            + midg[...]
-        ).astype(bf16)
-        out_copy(1, b).start()
         return carry
 
     lax.fori_loop(0, n_bucket, bucket, 0)
@@ -454,7 +457,9 @@
     keep_out[n_rows // 2 :, :] = total
     send_out[n_rows // 2 :, :] = total
     for i in range(len(outs)):
-        out_copy(i, n_bucket - 1).wait()
+        out_copy(i, 0).wait()
+    for c in folded_copies:
+        c.wait()
 
 
 def layer(lens, x, cot, ws, vecs, gains, shifts, down_t, up, wide):
@@ -472,6 +477,11 @@
     out_shape = [
         sds((t, d), bf16),
         sds((t, d), bf16),
+        sds((t, d), bf16),
+        sds((t, d), bf16),
+        sds((t, d), bf16),
+        sds((d, d), bf16),
+        sds((d, d), bf16),
         sds((n_rows // 2 + 8, LANES), f32),
         sds((n_rows // 2 + 8, LANES), f32),
     ]
@@ -501,7 +511,6 @@
         VMEM((BUCKET, ff), bf16),
         VMEM((BUCKET, d), bf16),
         VMEM((BUCKET, d), bf16),
-        VMEM((BUCKET, d), f32),
         VMEM((BUCKET, d), bf16),
         VMEM((BUCKET, d), bf16),
         VMEM((BUCKET, d), bf16),
@@ -511,18 +520,87 @@
         VMEM((n_rows, LANES), f32),
         dma((2 * n_bucket,)),
         dma((6,)),
-        dma((2,)),
+        dma((7,)),
     ]
     body = lambda *refs: layer_kernel(*refs, wide=wide)
     return pl.pallas_call(
         body,
         out_shape=out_shape,
         in_specs=in_specs,
-        out_specs=[any_spec] * 2 + [vm] * 2,
+        out_specs=[any_spec] * 7 + [vm] * 2,
         scratch_shapes=scratch,
         compiler_params=pltpu.CompilerParams(vmem_limit_bytes=63 << 20),
         name="layer",
     )(*ops)
+
+
+def token_kernel(*refs, first_row):
+    mg_hbm, dq_hbm, dk_hbm, dv_hbm, wq_hbm, wk_hbm, wv_hbm, out_hbm = refs[-16:-8]
+    mg, grads, weights, acc, out, g_sem, w_sem, m_sem = refs[-8:]
+    rows = mg.shape[0]
+    chunk = rows // 2
+    whole = slice(first_row, first_row + rows)
+    for i, (d_hbm, w_hbm) in enumerate(((dq_hbm, wq_hbm), (dk_hbm, wk_hbm), (dv_hbm, wv_hbm))):
+        pltpu.make_async_copy(w_hbm, weights.at[i], w_sem.at[i]).start()
+        pltpu.make_async_copy(d_hbm.at[whole, :], grads.at[i], g_sem.at[i]).start()
+    mid = pltpu.make_async_copy(mg_hbm.at[whole, :], mg, m_sem.at[0])
+    mid.start()
+
+    def side(i, carry):
+        pltpu.make_async_copy(wq_hbm, weights.at[i], w_sem.at[i]).wait()
+        pltpu.make_async_copy(dq_hbm.at[whole, :], grads.at[i], g_sem.at[i]).wait()
+        for c in range(2):
+            local = slice(c * chunk, (c + 1) * chunk)
+            part = cdot(grads[i, local, :], weights[i], 1, 1)
+            acc[local, :] = jnp.where(i == 0, part, acc[local, :] + part)
+        return carry
+
+    lax.fori_loop(0, 3, side, 0)
+    mid.wait()
+    writes = []
+    for c in range(2):
+        local = slice(c * chunk, (c + 1) * chunk)
+        out[local, :] = (acc[local, :] + mg[local, :].astype(f32)).astype(bf16)
+        at = slice(first_row + c * chunk, first_row + (c + 1) * chunk)
+        writes.append(
+            pltpu.make_async_copy(out.at[local, :], out_hbm.at[at, :], m_sem.at[1 + c])
+        )
+        writes[-1].start()
+    for w in writes:
+        w.wait()
+
+
+def token_gradient(prev, mg, dq, dk, dv, wq, wk, wv, first_row, rows):
+    t, d = mg.shape
+    any_spec = pl.BlockSpec(memory_space=pl.ANY)
+    args = (mg, dq, dk, dv, wq, wk, wv)
+    aliases = {}
+    if prev is not None:
+        args = (prev,) + args
+        aliases = {0: 0}
+    dma = pltpu.SemaphoreType.DMA
+    return pl.pallas_call(
+        lambda *refs: token_kernel(*refs, first_row=first_row),
+        out_shape=sds((t, d), bf16),
+        in_specs=[any_spec] * len(args),
+        out_specs=any_spec,
+        scratch_shapes=[
+            VMEM((rows, d), bf16),
+            VMEM((3, rows, d), bf16),
+            VMEM((3, d, d), bf16),
+            VMEM((rows, d), f32),
+            VMEM((rows, d), bf16),
+            dma((3,)),
+            dma((3,)),
+            dma((3,)),
+        ],
+        input_output_aliases=aliases,
+        compiler_params=pltpu.CompilerParams(vmem_limit_bytes=60 << 20),
+        cost_estimate=pl.CostEstimate(
+            flops=6 * rows * d * d, bytes_accessed=10 * rows * d, transcendentals=0
+        ),
+        name="token_gradient",
+    )(*args)
 
 
 def update_kernel(
@@ -684,7 +762,7 @@
     chunk_rows = n_rows // wide
 
     down_t = jnp.swapaxes(adapter_down_factors, 1, 2)
-    mixed, token_grad, keep, send = layer(
+    mixed, midg, dq, dk, dv, folded_q, folded_v, keep, send = layer(
         valid_token_length,
         tokens,
         cotangent,
@@ -710,9 +788,21 @@
         wide,
     )
 
+    def token_part(prev, after, first_row, rows):
+        held_back, _ = lax.optimization_barrier((midg, after))
+        return token_gradient(
+            prev, held_back, dq, dk, dv, folded_q, key_weight_matrix, folded_v, first_row, rows
+        )
+
+    n_tok = tokens.shape[0]
     grad = keep + lax.ppermute(send, "wide", swap_perm(wide, 1))
-    for group in digit_groups(dp, 0):
-        grad = tree_sum(exchange(grad, "dp", dp, group))
+    token_grad = token_part(None, grad, 0, n_tok // 2)
+    for i, group in enumerate(digit_groups(dp, 0)):
+        pieces = exchange(grad, "dp", dp, group)
+        if i == 0:
+            pieces, token_grad = lax.optimization_barrier((pieces, token_grad))
+        grad = tree_sum(pieces)
+    token_grad = token_part(token_grad, grad, n_tok // 2, n_tok // 2)
 
     first = first_moment_estimate.reshape(chunk_rows, LANES)
     second = second_moment_estimate.reshape(chunk_rows, LANES)
@@ -721,6 +811,8 @@
     groups = digit_groups(wide, 1)
     for i, (low, n) in enumerate(groups):
         pieces = exchange(jnp.concatenate([grad, first, second], axis=0), "wide", wide, (low, n))
+        if i == 0:
+            pieces, token_grad = lax.optimization_barrier((pieces, token_grad))
         grad = tree_sum([p[:rows] for p in pieces])
         if i + 1 < len(groups):
             block = held * chunk_rows

time: 113 us -> 107 us (0.947)
  waiting for transfers between devices: 11.2 us -> 1.41 us
  Pallas kernels: 87.6 us -> 92.4 us
    pallas_call x0 -> x2, Pallas kernels: none -> 12.3 us  [token_gradient(): pl.pallas_call(lambda *refs: token_kernel(*refs, first_row=first_row), ou...]
    ppermute x6, waiting for transfers between devices: 9.82 us -> 0.02 us  [exchange(): lax.ppermute(values, axis, swap_perm(size, j << low))]
    pallas_call x1, Pallas kernels: 86.2 us -> 78.6 us  [layer(): pl.pallas_call(body, out_shape=out_shape, in_specs=in_specs, out_specs=[a...]
  transfers between devices with their start and end apart: 8 -> 8, of which waited for: 6 -> 1; matrix products, arithmetic and copies ran while one was open for 0% -> 0% of each run, Pallas kernels for 0% -> 12%
where the time goes in v3:
time: 107 us
  Pallas kernels  92.4 us (86%)
  starting transfers between devices  9.52 us (9%)
  between operations  2.77 us (3%)
  waiting for transfers between devices  1.41 us (1%)
    pallas_call x1, Pallas kernels, layer(): pl.pallas_call(body, out_shape=out_shape, in_specs=in_specs, out_specs=[a...  78.6 us
    pallas_call x2, Pallas kernels, token_gradient(): pl.pallas_call(lambda *refs: token_kernel(*refs, first_row=first_row), ou...  12.3 us
    ppermute x6, starting transfers between devices, exchange(): lax.ppermute(values, axis, swap_perm(size, j << low))  7.47 us
  transfers between devices with their start and end apart: 8, of which 1 were waited for; matrix products, arithmetic and copies ran while one was open for 0% of the time, Pallas kernels for 12%

profile of v3, /device:TPU:1, one launch (start us, length us, event | category | flops | bytes accessed | tf_op | source)
XLA Modules:
  0.0 107.0 jit_solution(6670903303215119176)
XLA Ops:
  0.6 78.6 %layer.1 = (bf16[1536,768]{1,0:T(8,128)(2,1)}, bf16[1536,768]{1,0:T(8,128)(2,1)}, bf16[1536,768]{1,0:T(8,128)(2,1)}, bf16[1536,768]{1,0:T(8,128)(2,1)}, bf16[153...) custom-call(s32[7]{0:T(128)} %refs_0_.2, ...), custom_call_target="tpu_custom_call" | custom-call | tf_op jit(solution)/shard_map/layer/pallas_call | solution.py:526
  79.2 0.1 collective-permute-start
  79.4 1.4 %collective-permute-done = f32[104,128]{1,0:T(8,128)S(1)} collective-permute-done((f32[104,128]{1,0:T(8,128)}, f32[104,128]{1,0:T(8,128)S(1)}, u32[]{:S(2)}, u32[]{:S(2)}) %collective-permute-start) | collective-permute-done | bytes 53280 | tf_op jit(solution)/shard_map/ppermute | solution.py:798
  80.8 0.8 add.21
  81.6 2.4 %collective-permute-start.1 = (f32[104,128]{1,0:T(8,128)S(1)}, f32[104,128]{1,0:T(8,128)S(1)}, u32[]{:S(2)}, u32[]{:S(2)}) collective-permute-start(f32[104,128]{1,0:T(8,128)S(1)} %add.21), channel_id=1, source_target_pairs={{0,8},{8,0},{16,24},{24,16},{1,9},{9,1},{17,25},{25,17},{2,10},{10... | collective-permute-start | bytes 159752 | tf_op jit(solution)/shard_map/ppermute | solution.py:714
  83.9 1.2 %collective-permute-start.2 = (f32[104,128]{1,0:T(8,128)S(1)}, f32[104,128]{1,0:T(8,128)S(1)}, u32[]{:S(2)}, u32[]{:S(2)}) collective-permute-start(f32[104,128]{1,0:T(8,128)S(1)} %add.21), channel_id=1, source_target_pairs={{0,16},{8,24},{16,0},{24,8},{1,17},{9,25},{17,1},{25,9},{2,18},{10... | collective-permute-start | bytes 159752 | tf_op jit(solution)/shard_map/ppermute | solution.py:714
  85.2 0.0 collective-permute-start.3
  85.2 6.2 %token_gradient.2.refs_0_ = bf16[1536,768]{1,0:T(8,128)(2,1)} custom-call(bf16[1536,768]{1,0:T(8,128)(2,1)} %get-tuple-element.46.refs_0_.refs_1_, bf16[1536,768]{1,0:T(8,128)(2,1)} %get-tuple-element.36.refs_1_.refs_2_, bf16[1536,768]{1,0:T(8,128)(2,1)} %get-tuple-element.37.refs_2_.refs_3_, bf16[1536,768]{1,0:T(8,128)(2,1)} %get-tuple-element.38.refs_3_.refs_4_, ...), custom_call_target="tpu_custom_call" | custom-call | flops 2717908992 | bytes 5898240 | tf_op jit(solution)/shard_map/token_gradient/pallas_call | solution.py:582
  91.4 0.0 collective-permute-done.1
  91.4 0.0 collective-permute-done.2
  91.4 0.0 collective-permute-done.3
  91.4 0.0 copy-done.2
  91.5 0.0 copy-start
  91.5 0.0 copy-start.1
  91.5 1.5 %collective-permute-start.4 = (f32[152,128]{1,0:T(8,128)S(1)}, f32[152,128]{1,0:T(8,128)S(1)}, u32[]{:S(2)}, u32[]{:S(2)}) collective-permute-start(f32[152,128]{1,0:T(8,128)S(1)} %pad_maximum_fusion), channel_id=1, source_target_pairs={{0,2},{1,3},{2,0},{3,1},{4,6},{5,7},{6,4},{7,5},{8,10},{9,11},{10,... | collective-permute-start | bytes 233480 | tf_op jit(solution)/shard_map/ppermute | solution.py:714
  93.0 2.3 %collective-permute-start.5 = (f32[152,128]{1,0:T(8,128)S(1)}, f32[152,128]{1,0:T(8,128)S(1)}, u32[]{:S(2)}, u32[]{:S(2)}) collective-permute-start(f32[152,128]{1,0:T(8,128)S(1)} %pad_maximum_fusion), channel_id=1, source_target_pairs={{0,4},{1,5},{2,6},{3,7},{4,0},{5,1},{6,2},{7,3},{8,12},{9,13},{10,... | collective-permute-start | bytes 233480 | tf_op jit(solution)/shard_map/ppermute | solution.py:714
  95.3 0.0 collective-permute-start.6
  95.3 6.2 %token_gradient.3 = bf16[1536,768]{1,0:T(8,128)(2,1)} custom-call(bf16[1536,768]{1,0:T(8,128)(2,1)} %token_gradient.2.refs_0_, bf16[1536,768]{1,0:T(8,128)(2,1)} %get-tuple-element.46.refs_0_.refs_1_, bf16[1536,768]{1,0:T(8,128)(2,1)} %get-tuple-element.36.refs_1_.refs_2_, ...), custom_call_target="tpu_custom_call", output_to_operand_aliasing={{}: (0, {})} | custom-call | flops 2717908992 | bytes 5898240 | tf_op jit(solution)/shard_map/token_gradient/pallas_call | solution.py:582
  101.5 0.0 collective-permute-done.4
  101.5 0.0 collective-permute-done.5
  101.5 0.0 collective-permute-done.6
  101.6 1.9 %collective-permute-start.7 = (f32[296,128]{1,0:T(8,128)S(1)}, f32[296,128]{1,0:T(8,128)S(1)}, u32[]{:S(2)}, u32[]{:S(2)}) collective-permute-start(f32[296,128]{1,0:T(8,128)S(1)} %slice_dynamic-update-slice_fusion.refs_3_), channel_id=1, source_target_pairs={{0,1},{1,0},{2,3},{3,2},{4,5},{5,4},{6,7},{7,6},{8,9},{9,8},{10,11... | collective-permute-start | bytes 454664 | tf_op jit(solution)/shard_map/ppermute | solution.py:824
  105.5 0.0 collective-permute-done.7.refs_4_
  105.5 1.4 %update.1 = (f32[2,8,768]{2,1,0:T(8,128)}, f32[2,8,768]{2,1,0:T(8,128)}, f32[24,128]{1,0:T(8,128)}, f32[24,128]{1,0:T(8,128)}) custom-call(f32[1]{0:T(128)S(6)} %copy.35.refs_0_, f32[1]{0:T(128)S(6)} %copy.36.refs_1_, s32[1]{0:T(128)S(6)} %copy.37.refs_2_, f32[296,128]{1,0:T(8,128)S(1)} %slice_dynamic-update-slice_fusion.refs_3_, ...), custom_call_target="tpu_custom_call" | custom-call | tf_op jit(solution)/shard_map/update/pallas_call | solution.py:680
  (12 shorter events, 0.1 us)
Async XLA Ops:
  79.2 1.5 %collective-permute-start = (f32[104,128]{1,0:T(8,128)}, f32[104,128]{1,0:T(8,128)S(1)}, u32[]{:S(2)}, u32[]{:S(2)}) collective-permute-start(f32[104,128]{1,0:T(8,128)} %get-tuple-element.33), channel_id=1, source_target_pairs={{0,1},{1,0},{2,3},{3,2},{4,5},{5,4},{6,7},{7,6},{8,9},{9,8},{10,11... | collective-permute-start | bytes 159752 | tf_op jit(solution)/shard_map/ppermute | solution.py:798
  81.6 9.8 %collective-permute-start.1 = (f32[104,128]{1,0:T(8,128)S(1)}, f32[104,128]{1,0:T(8,128)S(1)}, u32[]{:S(2)}, u32[]{:S(2)}) collective-permute-start(f32[104,128]{1,0:T(8,128)S(1)} %add.21), channel_id=1, source_target_pairs={{0,8},{8,0},{16,24},{24,16},{1,9},{9,1},{17,25},{25,17},{2,10},{10... | collective-permute-start | bytes 159752 | tf_op jit(solution)/shard_map/ppermute | solution.py:714
  83.9 7.5 %collective-permute-start.2 = (f32[104,128]{1,0:T(8,128)S(1)}, f32[104,128]{1,0:T(8,128)S(1)}, u32[]{:S(2)}, u32[]{:S(2)}) collective-permute-start(f32[104,128]{1,0:T(8,128)S(1)} %add.21), channel_id=1, source_target_pairs={{0,16},{8,24},{16,0},{24,8},{1,17},{9,25},{17,1},{25,9},{2,18},{10... | collective-permute-start | bytes 159752 | tf_op jit(solution)/shard_map/ppermute | solution.py:714
  85.2 6.2 %collective-permute-start.3 = (f32[104,128]{1,0:T(8,128)S(1)}, f32[104,128]{1,0:T(8,128)S(1)}, u32[]{:S(2)}, u32[]{:S(2)}) collective-permute-start(f32[104,128]{1,0:T(8,128)S(1)} %add.21), channel_id=1, source_target_pairs={{0,24},{8,16},{16,8},{24,0},{1,25},{9,17},{17,9},{25,1},{2,26},{10... | collective-permute-start | bytes 159752 | tf_op jit(solution)/shard_map/ppermute | solution.py:714
  85.2 6.2 %copy-start.2 = (f32[3072]{0:T(1024)S(1)}, f32[3072]{0:T(1024)}, u32[]{:S(2)}) copy-start(f32[3072]{0:T(1024)} %param.42) | copy-start | bytes 36868
  85.2 6.2 %copy-start.3 = (f32[3072]{0:T(1024)S(1)}, f32[3072]{0:T(1024)}, u32[]{:S(2)}) copy-start(f32[3072]{0:T(1024)} %param.41) | copy-start | bytes 36868
  91.5 14.0 %copy-start = (f32[2,768,8]{1,2,0:T(8,128)S(1)}, f32[2,768,8]{1,2,0:T(8,128)}, u32[]{:S(2)}) copy-start(f32[2,768,8]{1,2,0:T(8,128)} %param.39) | copy-start | bytes 147460
  91.5 14.0 %copy-start.1 = (f32[2,8,768]{2,1,0:T(8,128)S(1)}, f32[2,8,768]{2,1,0:T(8,128)}, u32[]{:S(2)}) copy-start(f32[2,8,768]{2,1,0:T(8,128)} %refs_6_.5) | copy-start | bytes 147460
  91.5 10.0 %collective-permute-start.4 = (f32[152,128]{1,0:T(8,128)S(1)}, f32[152,128]{1,0:T(8,128)S(1)}, u32[]{:S(2)}, u32[]{:S(2)}) collective-permute-start(f32[152,128]{1,0:T(8,128)S(1)} %pad_maximum_fusion), channel_id=1, source_target_pairs={{0,2},{1,3},{2,0},{3,1},{4,6},{5,7},{6,4},{7,5},{8,10},{9,11},{10,... | collective-permute-start | bytes 233480 | tf_op jit(solution)/shard_map/ppermute | solution.py:714
  93.0 8.5 %collective-permute-start.5 = (f32[152,128]{1,0:T(8,128)S(1)}, f32[152,128]{1,0:T(8,128)S(1)}, u32[]{:S(2)}, u32[]{:S(2)}) collective-permute-start(f32[152,128]{1,0:T(8,128)S(1)} %pad_maximum_fusion), channel_id=1, source_target_pairs={{0,4},{1,5},{2,6},{3,7},{4,0},{5,1},{6,2},{7,3},{8,12},{9,13},{10,... | collective-permute-start | bytes 233480 | tf_op jit(solution)/shard_map/ppermute | solution.py:714
  95.3 6.2 %collective-permute-start.6 = (f32[152,128]{1,0:T(8,128)S(1)}, f32[152,128]{1,0:T(8,128)S(1)}, u32[]{:S(2)}, u32[]{:S(2)}) collective-permute-start(f32[152,128]{1,0:T(8,128)S(1)} %pad_maximum_fusion), channel_id=1, source_target_pairs={{0,6},{1,7},{2,4},{3,5},{4,2},{5,3},{6,0},{7,1},{8,14},{9,15},{10,... | collective-permute-start | bytes 233480 | tf_op jit(solution)/shard_map/ppermute | solution.py:714
  101.6 3.9 %collective-permute-start.7 = (f32[296,128]{1,0:T(8,128)S(1)}, f32[296,128]{1,0:T(8,128)S(1)}, u32[]{:S(2)}, u32[]{:S(2)}) collective-permute-start(f32[296,128]{1,0:T(8,128)S(1)} %slice_dynamic-update-slice_fusion.refs_3_), channel_id=1, source_target_pairs={{0,1},{1,0},{2,3},{3,2},{4,5},{5,4},{6,7},{7,6},{8,9},{9,8},{10,11... | collective-permute-start | bytes 454664 | tf_op jit(solution)/shard_map/ppermute | solution.py:824

commit v4 on v3

--- a/solution.py
+++ b/solution.py
@@ -72,7 +72,7 @@
     )
 
 
-def flatten_pair(flat, j, spread, up, scale):
+def flatten_pair(flat, j, spread, up):
     rank, width = up.shape
     group = LANES // rank
     down_rows = width // group
@@ -83,9 +83,7 @@
     up_rows = width // LANES
     base = 2 * down_rows + j * rank * up_rows
     for cb in range(up_rows):
-        flat[pl.ds(base + cb, rank, stride=up_rows), :] = (
-            scale * up[:, cb * LANES : (cb + 1) * LANES]
-        )
+        flat[pl.ds(base + cb, rank, stride=up_rows), :] = up[:, cb * LANES : (cb + 1) * LANES]
 
 
 def row_moves(wide, chunk_rows):
@@ -435,7 +433,7 @@
             axis=1,
         )
         g_down[...] += cdot(x[rows, :], dgb, 0, 0)
-        dnb2 = dn[...]
+        dnb2 = dn[:, : 2 * rank]
         g_up_q[...] += cdot(dnb2, dqb, 0, 0)
         g_up_v[...] += cdot(dnb2, dvb, 0, 0)
         return carry
@@ -448,7 +446,6 @@
             j,
             g_down[:, j * LANES : (j + 1) * LANES],
             src[j * rank : (j + 1) * rank, :],
-            adapter_scale,
         )
     n_rows = flat.shape[0]
     split_half(flat, keep_out, core, wide)
@@ -515,8 +512,8 @@
         VMEM((BUCKET, d), bf16),
         VMEM((BUCKET, d), bf16),
         VMEM((d, 2 * LANES), f32),
-        VMEM((LANES, d), f32),
-        VMEM((LANES, d), f32),
+        VMEM((2 * rank, d), f32),
+        VMEM((2 * rank, d), f32),
         VMEM((n_rows, LANES), f32),
         dma((2 * n_bucket,)),
         dma((6,)),
@@ -662,7 +659,12 @@
             moves[j * down_rows : (j + 1) * down_rows, :][:, None, :], (down_rows, group, LANES)
         ).reshape(width, LANES)
         part = jnp.where(lane_is_feature(width, rank), spread, 0.0)
-        move = cdot(lane_is_rank(rank).astype(f32), part, 1, 1, lax.Precision.HIGHEST)
+        pick = lane_is_rank(rank).astype(bf16)
+        high = part.astype(bf16)
+        rest = part - high.astype(f32)
+        middle = rest.astype(bf16)
+        low_part = (rest - middle.astype(f32)).astype(bf16)
+        move = cdot(pick, high, 1, 1) + cdot(pick, middle, 1, 1) + cdot(pick, low_part, 1, 1)
         new_down_t[j] = down_t[j] * (1.0 - rate_first * decay_first) - rate_first * move
         base = 2 * down_rows + j * rank * up_rows
         for cb in range(up_rows):
@@ -795,7 +797,11 @@
         )
 
     n_tok = tokens.shape[0]
-    grad = keep + lax.ppermute(send, "wide", swap_perm(wide, 1))
+    row = lax.broadcasted_iota(jnp.int32, keep.shape, 0)
+    is_up = (row >= n_rows // 4) & (row < n_rows // 2)
+    scale = jnp.where(is_up, adapter_scale, 1.0)
+    kept = lax.optimization_barrier(keep * scale)
+    grad = kept + lax.ppermute(send, "wide", swap_perm(wide, 1)) * scale
     token_grad = token_part(None, grad, 0, n_tok // 2)
     for i, group in enumerate(digit_groups(dp, 0)):
         pieces = exchange(grad, "dp", dp, group)

time: 107 us -> 106 us (level)
  transfers between devices with their start and end apart: 8 -> 8, of which waited for: 1 -> 1; matrix products, arithmetic and copies ran while one was open for 0% -> 1% of each run, Pallas kernels for 12% -> 12%
where the time goes in v4:
time: 106 us
  Pallas kernels  92.1 us (87%)
  starting transfers between devices  9.59 us (9%)
  between operations  2.78 us (3%)
    pallas_call x1, Pallas kernels, layer(): pl.pallas_call(body, out_shape=out_shape, in_specs=in_specs, out_specs=[a...  78.6 us
    pallas_call x2, Pallas kernels, token_gradient(): pl.pallas_call(lambda *refs: token_kernel(*refs, first_row=first_row), ou...  12.3 us
    ppermute x6, starting transfers between devices, exchange(): lax.ppermute(values, axis, swap_perm(size, j << low))  7.54 us
  transfers between devices with their start and end apart: 8, of which 1 were waited for; matrix products, arithmetic and copies ran while one was open for 1% of the time, Pallas kernels for 12%

profile of v4, /device:TPU:1, one launch (start us, length us, event | category | flops | bytes accessed | tf_op | source)
XLA Modules:
  0.0 106.1 jit_solution(1263166161931112608)
XLA Ops:
  0.6 78.6 %layer.1 = (bf16[1536,768]{1,0:T(8,128)(2,1)}, bf16[1536,768]{1,0:T(8,128)(2,1)}, bf16[1536,768]{1,0:T(8,128)(2,1)}, bf16[1536,768]{1,0:T(8,128)(2,1)}, bf16[153...) custom-call(s32[7]{0:T(128)} %refs_0_.2, ...), custom_call_target="tpu_custom_call" | custom-call | tf_op jit(solution)/shard_map/layer/pallas_call | solution.py:523
  79.3 0.1 collective-permute-start
  79.4 0.9 broadcast_multiply_fusion
  80.3 0.5 collective-permute-done
  80.8 0.1 multiply_add_fusion
  80.9 2.4 %collective-permute-start.1 = (f32[104,128]{1,0:T(8,128)S(1)}, f32[104,128]{1,0:T(8,128)S(1)}, u32[]{:S(2)}, u32[]{:S(2)}) collective-permute-start(f32[104,128]{1,0:T(8,128)S(1)} %multiply_add_fusion), channel_id=1, source_target_pairs={{0,8},{8,0},{16,24},{24,16},{1,9},{9,1},{17,25},{25,17},{2,10},{10... | collective-permute-start | bytes 159752 | tf_op jit(solution)/shard_map/ppermute | solution.py:716
  83.3 1.2 %collective-permute-start.2 = (f32[104,128]{1,0:T(8,128)S(1)}, f32[104,128]{1,0:T(8,128)S(1)}, u32[]{:S(2)}, u32[]{:S(2)}) collective-permute-start(f32[104,128]{1,0:T(8,128)S(1)} %multiply_add_fusion), channel_id=1, source_target_pairs={{0,16},{8,24},{16,0},{24,8},{1,17},{9,25},{17,1},{25,9},{2,18},{10... | collective-permute-start | bytes 159752 | tf_op jit(solution)/shard_map/ppermute | solution.py:716
  84.5 0.0 collective-permute-start.3
  84.6 6.2 %token_gradient.2.refs_0_ = bf16[1536,768]{1,0:T(8,128)(2,1)} custom-call(bf16[1536,768]{1,0:T(8,128)(2,1)} %get-tuple-element.46.refs_0_.refs_1_, bf16[1536,768]{1,0:T(8,128)(2,1)} %get-tuple-element.36.refs_1_.refs_2_, bf16[1536,768]{1,0:T(8,128)(2,1)} %get-tuple-element.37.refs_2_.refs_3_, bf16[1536,768]{1,0:T(8,128)(2,1)} %get-tuple-element.38.refs_3_.refs_4_, ...), custom_call_target="tpu_custom_call" | custom-call | flops 2717908992 | bytes 5898240 | tf_op jit(solution)/shard_map/token_gradient/pallas_call | solution.py:579
  90.7 0.0 collective-permute-done.1
  90.7 0.0 collective-permute-done.2
  90.8 0.0 collective-permute-done.3
  90.8 0.0 copy-start
  90.8 0.0 copy-start.1
  90.8 1.5 %collective-permute-start.4 = (f32[152,128]{1,0:T(8,128)S(1)}, f32[152,128]{1,0:T(8,128)S(1)}, u32[]{:S(2)}, u32[]{:S(2)}) collective-permute-start(f32[152,128]{1,0:T(8,128)S(1)} %pad_maximum_fusion), channel_id=1, source_target_pairs={{0,2},{1,3},{2,0},{3,1},{4,6},{5,7},{6,4},{7,5},{8,10},{9,11},{10,... | collective-permute-start | bytes 233480 | tf_op jit(solution)/shard_map/ppermute | solution.py:716
  92.4 2.3 %collective-permute-start.5 = (f32[152,128]{1,0:T(8,128)S(1)}, f32[152,128]{1,0:T(8,128)S(1)}, u32[]{:S(2)}, u32[]{:S(2)}) collective-permute-start(f32[152,128]{1,0:T(8,128)S(1)} %pad_maximum_fusion), channel_id=1, source_target_pairs={{0,4},{1,5},{2,6},{3,7},{4,0},{5,1},{6,2},{7,3},{8,12},{9,13},{10,... | collective-permute-start | bytes 233480 | tf_op jit(solution)/shard_map/ppermute | solution.py:716
  94.7 0.0 collective-permute-start.6
  94.7 6.2 %token_gradient.3 = bf16[1536,768]{1,0:T(8,128)(2,1)} custom-call(bf16[1536,768]{1,0:T(8,128)(2,1)} %token_gradient.2.refs_0_, bf16[1536,768]{1,0:T(8,128)(2,1)} %get-tuple-element.46.refs_0_.refs_1_, bf16[1536,768]{1,0:T(8,128)(2,1)} %get-tuple-element.36.refs_1_.refs_2_, ...), custom_call_target="tpu_custom_call", output_to_operand_aliasing={{}: (0, {})} | custom-call | flops 2717908992 | bytes 5898240 | tf_op jit(solution)/shard_map/token_gradient/pallas_call | solution.py:579
  100.9 0.0 collective-permute-done.4
  100.9 0.0 collective-permute-done.5
  100.9 0.0 collective-permute-done.6
  101.0 1.9 %collective-permute-start.7 = (f32[296,128]{1,0:T(8,128)S(1)}, f32[296,128]{1,0:T(8,128)S(1)}, u32[]{:S(2)}, u32[]{:S(2)}) collective-permute-start(f32[296,128]{1,0:T(8,128)S(1)} %slice_dynamic-update-slice_fusion.refs_3_), channel_id=1, source_target_pairs={{0,1},{1,0},{2,3},{3,2},{4,5},{5,4},{6,7},{7,6},{8,9},{9,8},{10,11... | collective-permute-start | bytes 454664 | tf_op jit(solution)/shard_map/ppermute | solution.py:830
  104.8 0.0 collective-permute-done.7.refs_4_
  104.9 1.2 %update.1 = (f32[2,8,768]{2,1,0:T(8,128)}, f32[2,8,768]{2,1,0:T(8,128)}, f32[24,128]{1,0:T(8,128)}, f32[24,128]{1,0:T(8,128)}) custom-call(f32[1]{0:T(128)S(6)} %copy.35.refs_0_, f32[1]{0:T(128)S(6)} %copy.36.refs_1_, s32[1]{0:T(128)S(6)} %copy.37.refs_2_, f32[296,128]{1,0:T(8,128)S(1)} %slice_dynamic-update-slice_fusion.refs_3_, ...), custom_call_target="tpu_custom_call" | custom-call | tf_op jit(solution)/shard_map/update/pallas_call | solution.py:682
  (14 shorter events, 0.1 us)
Async XLA Ops:
  79.3 1.5 %collective-permute-start = (f32[104,128]{1,0:T(8,128)}, f32[104,128]{1,0:T(8,128)S(1)}, u32[]{:S(2)}, u32[]{:S(2)}) collective-permute-start(f32[104,128]{1,0:T(8,128)} %get-tuple-element.33), channel_id=1, source_target_pairs={{0,1},{1,0},{2,3},{3,2},{4,5},{5,4},{6,7},{7,6},{8,9},{9,8},{10,11... | collective-permute-start | bytes 159752 | tf_op jit(solution)/shard_map/ppermute | solution.py:804
  80.9 9.9 %collective-permute-start.1 = (f32[104,128]{1,0:T(8,128)S(1)}, f32[104,128]{1,0:T(8,128)S(1)}, u32[]{:S(2)}, u32[]{:S(2)}) collective-permute-start(f32[104,128]{1,0:T(8,128)S(1)} %multiply_add_fusion), channel_id=1, source_target_pairs={{0,8},{8,0},{16,24},{24,16},{1,9},{9,1},{17,25},{25,17},{2,10},{10... | collective-permute-start | bytes 159752 | tf_op jit(solution)/shard_map/ppermute | solution.py:716
  83.3 7.5 %collective-permute-start.2 = (f32[104,128]{1,0:T(8,128)S(1)}, f32[104,128]{1,0:T(8,128)S(1)}, u32[]{:S(2)}, u32[]{:S(2)}) collective-permute-start(f32[104,128]{1,0:T(8,128)S(1)} %multiply_add_fusion), channel_id=1, source_target_pairs={{0,16},{8,24},{16,0},{24,8},{1,17},{9,25},{17,1},{25,9},{2,18},{10... | collective-permute-start | bytes 159752 | tf_op jit(solution)/shard_map/ppermute | solution.py:716
  84.5 6.2 %collective-permute-start.3 = (f32[104,128]{1,0:T(8,128)S(1)}, f32[104,128]{1,0:T(8,128)S(1)}, u32[]{:S(2)}, u32[]{:S(2)}) collective-permute-start(f32[104,128]{1,0:T(8,128)S(1)} %multiply_add_fusion), channel_id=1, source_target_pairs={{0,24},{8,16},{16,8},{24,0},{1,25},{9,17},{17,9},{25,1},{2,26},{10... | collective-permute-start | bytes 159752 | tf_op jit(solution)/shard_map/ppermute | solution.py:716
  84.5 6.2 %copy-start.2 = (f32[3072]{0:T(1024)S(1)}, f32[3072]{0:T(1024)}, u32[]{:S(2)}) copy-start(f32[3072]{0:T(1024)} %param.42) | copy-start | bytes 36868
  84.6 6.2 %copy-start.3 = (f32[3072]{0:T(1024)S(1)}, f32[3072]{0:T(1024)}, u32[]{:S(2)}) copy-start(f32[3072]{0:T(1024)} %param.41) | copy-start | bytes 36868
  90.8 14.0 %copy-start = (f32[2,768,8]{1,2,0:T(8,128)S(1)}, f32[2,768,8]{1,2,0:T(8,128)}, u32[]{:S(2)}) copy-start(f32[2,768,8]{1,2,0:T(8,128)} %param.39) | copy-start | bytes 147460
  90.8 14.0 %copy-start.1 = (f32[2,8,768]{2,1,0:T(8,128)S(1)}, f32[2,8,768]{2,1,0:T(8,128)}, u32[]{:S(2)}) copy-start(f32[2,8,768]{2,1,0:T(8,128)} %refs_6_.5) | copy-start | bytes 147460
  90.8 10.0 %collective-permute-start.4 = (f32[152,128]{1,0:T(8,128)S(1)}, f32[152,128]{1,0:T(8,128)S(1)}, u32[]{:S(2)}, u32[]{:S(2)}) collective-permute-start(f32[152,128]{1,0:T(8,128)S(1)} %pad_maximum_fusion), channel_id=1, source_target_pairs={{0,2},{1,3},{2,0},{3,1},{4,6},{5,7},{6,4},{7,5},{8,10},{9,11},{10,... | collective-permute-start | bytes 233480 | tf_op jit(solution)/shard_map/ppermute | solution.py:716
  92.4 8.5 %collective-permute-start.5 = (f32[152,128]{1,0:T(8,128)S(1)}, f32[152,128]{1,0:T(8,128)S(1)}, u32[]{:S(2)}, u32[]{:S(2)}) collective-permute-start(f32[152,128]{1,0:T(8,128)S(1)} %pad_maximum_fusion), channel_id=1, source_target_pairs={{0,4},{1,5},{2,6},{3,7},{4,0},{5,1},{6,2},{7,3},{8,12},{9,13},{10,... | collective-permute-start | bytes 233480 | tf_op jit(solution)/shard_map/ppermute | solution.py:716
  94.7 6.2 %collective-permute-start.6 = (f32[152,128]{1,0:T(8,128)S(1)}, f32[152,128]{1,0:T(8,128)S(1)}, u32[]{:S(2)}, u32[]{:S(2)}) collective-permute-start(f32[152,128]{1,0:T(8,128)S(1)} %pad_maximum_fusion), channel_id=1, source_target_pairs={{0,6},{1,7},{2,4},{3,5},{4,2},{5,3},{6,0},{7,1},{8,14},{9,15},{10,... | collective-permute-start | bytes 233480 | tf_op jit(solution)/shard_map/ppermute | solution.py:716
  101.0 3.9 %collective-permute-start.7 = (f32[296,128]{1,0:T(8,128)S(1)}, f32[296,128]{1,0:T(8,128)S(1)}, u32[]{:S(2)}, u32[]{:S(2)}) collective-permute-start(f32[296,128]{1,0:T(8,128)S(1)} %slice_dynamic-update-slice_fusion.refs_3_), channel_id=1, source_target_pairs={{0,1},{1,0},{2,3},{3,2},{4,5},{5,4},{6,7},{7,6},{8,9},{9,8},{10,11... | collective-permute-start | bytes 454664 | tf_op jit(solution)/shard_map/ppermute | solution.py:830

commit v5 on v4

--- a/solution.py
+++ b/solution.py
@@ -184,8 +184,8 @@
     x_copies = [bucket_copy(i, x_hbm, x, in_sem.at[i]) for i in range(n_bucket)]
     cot_copies = [bucket_copy(i, cot_hbm, cot, in_sem.at[n_bucket + i]) for i in range(n_bucket)]
     x_copies[-1].start()
-    for c in weight_copies[:4]:
-        c.start()
+    for i in (0, 2, 1, 3):
+        weight_copies[i].start()
     cot_copies[-1].start()
     for c in weight_copies[4:]:
         c.start()
@@ -351,10 +351,18 @@
         return pltpu.make_async_copy(src, dst.at[rows, :], out_sem.at[i])
 
     def out_free(which, b):
-        @pl.when(b < n_bucket - 1)
-        def _():
+        if b < n_bucket - 1:
             for i in which:
                 out_copy(i, b + 1).wait()
+
+    for i, w, low, high in ((0, wq, down_t[0], up_q), (2, wv, down_t[1], up_v)):
+        weight_copies[i].wait()
+        w[...] = (
+            w[...].astype(f32) + cdot(low.astype(bf16), high.astype(bf16), 0, 0)
+        ).astype(bf16)
+    weight_copies[1].wait()
+    for c in folded_copies:
+        c.start()
 
     def bucket(step_b, carry):
         b = n_bucket - 1 - step_b
@@ -364,17 +372,6 @@
             pltpu.make_async_copy(src.at[rows, :], dst.at[rows, :], in_sem.at[base + b]).wait()
 
         wait_bucket(x_hbm, x, 0)
-
-        @pl.when(step_b == 0)
-        def _():
-            for i, (w, low, high) in enumerate(((wq, down_t[0], up_q), (wk, None, None), (wv, down_t[1], up_v))):
-                weight_copies[i].wait()
-                if low is not None:
-                    w[...] = (
-                        w[...].astype(f32) + cdot(low.astype(bf16), high.astype(bf16), 0, 0)
-                    ).astype(bf16)
-            for c in folded_copies:
-                c.start()
 
         xb = x[rows, :]
         dnb = cdot(xb, acat[...], 1, 1).astype(bf16)
@@ -396,28 +393,25 @@
                         attend(length, first, p, s)
 
                 each_pair(ahead[i], both)
+                wait_bucket(cot_hbm, cot, n_bucket)
+                out_free((0, 1), i)
+                if i == n_bucket - 1:
+                    for c in weight_copies[3:]:
+                        c.wait()
 
             first += count
-
-        wait_bucket(cot_hbm, cot, n_bucket)
-
-        @pl.when(step_b == 0)
-        def _():
-            for c in weight_copies[3:]:
-                c.wait()
-
-        out_free((0, 1), b)
 
         chain(b)
         for i in (0, 1):
             out_copy(i, b).start()
-        out_free((2, 3, 4), b)
 
         for i, length in enumerate((LEN_A, LEN_B, LEN_C)):
             count = BUCKET // length
 
             @pl.when(b == i)
             def _(i=i, length=length, count=count):
+                out_free((2, 3, 4), i)
+
                 def both(p, place):
                     for s in range(count):
                         attend_back(length, p, s, (place * count + s) % 2 == 1)
@@ -552,12 +546,19 @@
             acc[local, :] = jnp.where(i == 0, part, acc[local, :] + part)
         return carry
 
-    lax.fori_loop(0, 3, side, 0)
+    whole_loop = first_row > 0
+    lax.fori_loop(0, 3 if whole_loop else 2, side, 0)
+    if not whole_loop:
+        pltpu.make_async_copy(wq_hbm, weights.at[2], w_sem.at[2]).wait()
+        pltpu.make_async_copy(dq_hbm.at[whole, :], grads.at[2], g_sem.at[2]).wait()
     mid.wait()
     writes = []
     for c in range(2):
         local = slice(c * chunk, (c + 1) * chunk)
-        out[local, :] = (acc[local, :] + mg[local, :].astype(f32)).astype(bf16)
+        total = acc[local, :]
+        if not whole_loop:
+            total = total + cdot(grads[2, local, :], weights[2], 1, 1)
+        out[local, :] = (total + mg[local, :].astype(f32)).astype(bf16)
         at = slice(first_row + c * chunk, first_row + (c + 1) * chunk)
         writes.append(
             pltpu.make_async_copy(out.at[local, :], out_hbm.at[at, :], m_sem.at[1 + c])

time: 106 us -> 106 us (level)
  transfers between devices with their start and end apart: 8 -> 8, of which waited for: 1 -> 1; matrix products, arithmetic and copies ran while one was open for 1% -> 1% of each run, Pallas kernels for 12% -> 11%
where the time goes in v5:
time: 106 us; the launch traced here: 105 us
  Pallas kernels  91.5 us (86%)
  starting transfers between devices  9.55 us (9%)
  between operations  2.78 us (3%)
    pallas_call x1, Pallas kernels, layer(): pl.pallas_call(body, out_shape=out_shape, in_specs=in_specs, out_specs=[a...  78.3 us
    pallas_call x2, Pallas kernels, token_gradient(): pl.pallas_call(lambda *refs: token_kernel(*refs, first_row=first_row), ou...  12.1 us
    ppermute x6, starting transfers between devices, exchange(): lax.ppermute(values, axis, swap_perm(size, j << low))  7.53 us
  transfers between devices with their start and end apart: 8, of which 1 were waited for; matrix products, arithmetic and copies ran while one was open for 1% of the time, Pallas kernels for 11%

profile of v5, /device:TPU:1, one launch (start us, length us, event | category | flops | bytes accessed | tf_op | source)
XLA Modules:
  0.0 105.4 jit_solution(1603679283403212785)
XLA Ops:
  0.6 78.3 %layer.1 = (bf16[1536,768]{1,0:T(8,128)(2,1)}, bf16[1536,768]{1,0:T(8,128)(2,1)}, bf16[1536,768]{1,0:T(8,128)(2,1)}, bf16[1536,768]{1,0:T(8,128)(2,1)}, bf16[153...) custom-call(s32[7]{0:T(128)} %refs_0_.2, ...), custom_call_target="tpu_custom_call" | custom-call | tf_op jit(solution)/shard_map/layer/pallas_call | solution.py:517
  78.9 0.1 collective-permute-start
  79.0 0.9 broadcast_multiply_fusion
  79.9 0.5 collective-permute-done
  80.4 0.1 multiply_add_fusion
  80.5 2.4 %collective-permute-start.1 = (f32[104,128]{1,0:T(8,128)S(1)}, f32[104,128]{1,0:T(8,128)S(1)}, u32[]{:S(2)}, u32[]{:S(2)}) collective-permute-start(f32[104,128]{1,0:T(8,128)S(1)} %multiply_add_fusion), channel_id=1, source_target_pairs={{0,8},{8,0},{16,24},{24,16},{1,9},{9,1},{17,25},{25,17},{2,10},{10... | collective-permute-start | bytes 159752 | tf_op jit(solution)/shard_map/ppermute | solution.py:717
  82.9 1.3 %collective-permute-start.2 = (f32[104,128]{1,0:T(8,128)S(1)}, f32[104,128]{1,0:T(8,128)S(1)}, u32[]{:S(2)}, u32[]{:S(2)}) collective-permute-start(f32[104,128]{1,0:T(8,128)S(1)} %multiply_add_fusion), channel_id=1, source_target_pairs={{0,16},{8,24},{16,0},{24,8},{1,17},{9,25},{17,1},{25,9},{2,18},{10... | collective-permute-start | bytes 159752 | tf_op jit(solution)/shard_map/ppermute | solution.py:717
  84.2 0.0 collective-permute-start.3
  84.2 5.9 %token_gradient.2.refs_0_ = bf16[1536,768]{1,0:T(8,128)(2,1)} custom-call(bf16[1536,768]{1,0:T(8,128)(2,1)} %get-tuple-element.46.refs_0_.refs_1_, bf16[1536,768]{1,0:T(8,128)(2,1)} %get-tuple-element.36.refs_1_.refs_2_, bf16[1536,768]{1,0:T(8,128)(2,1)} %get-tuple-element.37.refs_2_.refs_3_, bf16[1536,768]{1,0:T(8,128)(2,1)} %get-tuple-element.38.refs_3_.refs_4_, ...), custom_call_target="tpu_custom_call" | custom-call | flops 2717908992 | bytes 5898240 | tf_op jit(solution)/shard_map/token_gradient/pallas_call | solution.py:580
  90.1 0.0 collective-permute-done.1
  90.1 0.0 collective-permute-done.2
  90.1 0.0 collective-permute-done.3
  90.2 0.0 copy-start
  90.2 0.0 copy-start.1
  90.2 1.5 %collective-permute-start.4 = (f32[152,128]{1,0:T(8,128)S(1)}, f32[152,128]{1,0:T(8,128)S(1)}, u32[]{:S(2)}, u32[]{:S(2)}) collective-permute-start(f32[152,128]{1,0:T(8,128)S(1)} %pad_maximum_fusion), channel_id=1, source_target_pairs={{0,2},{1,3},{2,0},{3,1},{4,6},{5,7},{6,4},{7,5},{8,10},{9,11},{10,... | collective-permute-start | bytes 233480 | tf_op jit(solution)/shard_map/ppermute | solution.py:717
  91.8 2.3 %collective-permute-start.5 = (f32[152,128]{1,0:T(8,128)S(1)}, f32[152,128]{1,0:T(8,128)S(1)}, u32[]{:S(2)}, u32[]{:S(2)}) collective-permute-start(f32[152,128]{1,0:T(8,128)S(1)} %pad_maximum_fusion), channel_id=1, source_target_pairs={{0,4},{1,5},{2,6},{3,7},{4,0},{5,1},{6,2},{7,3},{8,12},{9,13},{10,... | collective-permute-start | bytes 233480 | tf_op jit(solution)/shard_map/ppermute | solution.py:717
  94.1 0.0 collective-permute-start.6
  94.1 6.2 %token_gradient.3 = bf16[1536,768]{1,0:T(8,128)(2,1)} custom-call(bf16[1536,768]{1,0:T(8,128)(2,1)} %token_gradient.2.refs_0_, bf16[1536,768]{1,0:T(8,128)(2,1)} %get-tuple-element.46.refs_0_.refs_1_, bf16[1536,768]{1,0:T(8,128)(2,1)} %get-tuple-element.36.refs_1_.refs_2_, ...), custom_call_target="tpu_custom_call", output_to_operand_aliasing={{}: (0, {})} | custom-call | flops 2717908992 | bytes 5898240 | tf_op jit(solution)/shard_map/token_gradient/pallas_call | solution.py:580
  100.2 0.0 collective-permute-done.4
  100.2 0.0 collective-permute-done.5
  100.3 0.0 collective-permute-done.6
  100.3 1.9 %collective-permute-start.7 = (f32[296,128]{1,0:T(8,128)S(1)}, f32[296,128]{1,0:T(8,128)S(1)}, u32[]{:S(2)}, u32[]{:S(2)}) collective-permute-start(f32[296,128]{1,0:T(8,128)S(1)} %slice_dynamic-update-slice_fusion.refs_3_), channel_id=1, source_target_pairs={{0,1},{1,0},{2,3},{3,2},{4,5},{5,4},{6,7},{7,6},{8,9},{9,8},{10,11... | collective-permute-start | bytes 454664 | tf_op jit(solution)/shard_map/ppermute | solution.py:831
  104.2 0.0 collective-permute-done.7.refs_4_
  104.2 1.2 %update.1 = (f32[2,8,768]{2,1,0:T(8,128)}, f32[2,8,768]{2,1,0:T(8,128)}, f32[24,128]{1,0:T(8,128)}, f32[24,128]{1,0:T(8,128)}) custom-call(f32[1]{0:T(128)S(6)} %copy.35.refs_0_, f32[1]{0:T(128)S(6)} %copy.36.refs_1_, s32[1]{0:T(128)S(6)} %copy.37.refs_2_, f32[296,128]{1,0:T(8,128)S(1)} %slice_dynamic-update-slice_fusion.refs_3_, ...), custom_call_target="tpu_custom_call" | custom-call | tf_op jit(solution)/shard_map/update/pallas_call | solution.py:683
  (14 shorter events, 0.1 us)
Async XLA Ops:
  78.9 1.5 %collective-permute-start = (f32[104,128]{1,0:T(8,128)}, f32[104,128]{1,0:T(8,128)S(1)}, u32[]{:S(2)}, u32[]{:S(2)}) collective-permute-start(f32[104,128]{1,0:T(8,128)} %get-tuple-element.33), channel_id=1, source_target_pairs={{0,1},{1,0},{2,3},{3,2},{4,5},{5,4},{6,7},{7,6},{8,9},{9,8},{10,11... | collective-permute-start | bytes 159752 | tf_op jit(solution)/shard_map/ppermute | solution.py:805
  80.5 9.6 %collective-permute-start.1 = (f32[104,128]{1,0:T(8,128)S(1)}, f32[104,128]{1,0:T(8,128)S(1)}, u32[]{:S(2)}, u32[]{:S(2)}) collective-permute-start(f32[104,128]{1,0:T(8,128)S(1)} %multiply_add_fusion), channel_id=1, source_target_pairs={{0,8},{8,0},{16,24},{24,16},{1,9},{9,1},{17,25},{25,17},{2,10},{10... | collective-permute-start | bytes 159752 | tf_op jit(solution)/shard_map/ppermute | solution.py:717
  82.9 7.2 %collective-permute-start.2 = (f32[104,128]{1,0:T(8,128)S(1)}, f32[104,128]{1,0:T(8,128)S(1)}, u32[]{:S(2)}, u32[]{:S(2)}) collective-permute-start(f32[104,128]{1,0:T(8,128)S(1)} %multiply_add_fusion), channel_id=1, source_target_pairs={{0,16},{8,24},{16,0},{24,8},{1,17},{9,25},{17,1},{25,9},{2,18},{10... | collective-permute-start | bytes 159752 | tf_op jit(solution)/shard_map/ppermute | solution.py:717
  84.2 5.9 %collective-permute-start.3 = (f32[104,128]{1,0:T(8,128)S(1)}, f32[104,128]{1,0:T(8,128)S(1)}, u32[]{:S(2)}, u32[]{:S(2)}) collective-permute-start(f32[104,128]{1,0:T(8,128)S(1)} %multiply_add_fusion), channel_id=1, source_target_pairs={{0,24},{8,16},{16,8},{24,0},{1,25},{9,17},{17,9},{25,1},{2,26},{10... | collective-permute-start | bytes 159752 | tf_op jit(solution)/shard_map/ppermute | solution.py:717
  84.2 6.0 %copy-start.2 = (f32[3072]{0:T(1024)S(1)}, f32[3072]{0:T(1024)}, u32[]{:S(2)}) copy-start(f32[3072]{0:T(1024)} %param.42) | copy-start | bytes 36868
  84.2 6.0 %copy-start.3 = (f32[3072]{0:T(1024)S(1)}, f32[3072]{0:T(1024)}, u32[]{:S(2)}) copy-start(f32[3072]{0:T(1024)} %param.41) | copy-start | bytes 36868
  90.2 14.0 %copy-start = (f32[2,768,8]{1,2,0:T(8,128)S(1)}, f32[2,768,8]{1,2,0:T(8,128)}, u32[]{:S(2)}) copy-start(f32[2,768,8]{1,2,0:T(8,128)} %param.39) | copy-start | bytes 147460
  90.2 14.0 %copy-start.1 = (f32[2,8,768]{2,1,0:T(8,128)S(1)}, f32[2,8,768]{2,1,0:T(8,128)}, u32[]{:S(2)}) copy-start(f32[2,8,768]{2,1,0:T(8,128)} %refs_6_.5) | copy-start | bytes 147460
  90.2 10.0 %collective-permute-start.4 = (f32[152,128]{1,0:T(8,128)S(1)}, f32[152,128]{1,0:T(8,128)S(1)}, u32[]{:S(2)}, u32[]{:S(2)}) collective-permute-start(f32[152,128]{1,0:T(8,128)S(1)} %pad_maximum_fusion), channel_id=1, source_target_pairs={{0,2},{1,3},{2,0},{3,1},{4,6},{5,7},{6,4},{7,5},{8,10},{9,11},{10,... | collective-permute-start | bytes 233480 | tf_op jit(solution)/shard_map/ppermute | solution.py:717
  91.8 8.5 %collective-permute-start.5 = (f32[152,128]{1,0:T(8,128)S(1)}, f32[152,128]{1,0:T(8,128)S(1)}, u32[]{:S(2)}, u32[]{:S(2)}) collective-permute-start(f32[152,128]{1,0:T(8,128)S(1)} %pad_maximum_fusion), channel_id=1, source_target_pairs={{0,4},{1,5},{2,6},{3,7},{4,0},{5,1},{6,2},{7,3},{8,12},{9,13},{10,... | collective-permute-start | bytes 233480 | tf_op jit(solution)/shard_map/ppermute | solution.py:717
  94.1 6.2 %collective-permute-start.6 = (f32[152,128]{1,0:T(8,128)S(1)}, f32[152,128]{1,0:T(8,128)S(1)}, u32[]{:S(2)}, u32[]{:S(2)}) collective-permute-start(f32[152,128]{1,0:T(8,128)S(1)} %pad_maximum_fusion), channel_id=1, source_target_pairs={{0,6},{1,7},{2,4},{3,5},{4,2},{5,3},{6,0},{7,1},{8,14},{9,15},{10,... | collective-permute-start | bytes 233480 | tf_op jit(solution)/shard_map/ppermute | solution.py:717
  100.3 3.9 %collective-permute-start.7 = (f32[296,128]{1,0:T(8,128)S(1)}, f32[296,128]{1,0:T(8,128)S(1)}, u32[]{:S(2)}, u32[]{:S(2)}) collective-permute-start(f32[296,128]{1,0:T(8,128)S(1)} %slice_dynamic-update-slice_fusion.refs_3_), channel_id=1, source_target_pairs={{0,1},{1,0},{2,3},{3,2},{4,5},{5,4},{6,7},{7,6},{8,9},{9,8},{10,11... | collective-permute-start | bytes 454664 | tf_op jit(solution)/shard_map/ppermute | solution.py:831
